TPU v7x, 256 devices: a whole 4x4x8 slice. The times are simulated.
256 devices in a mesh: section: 8 (over z), expert: 8 (over y_hi, x), dp: 4 (over y_lo, core).
Axes of the slice: x: 4, y: 4 (y_hi: 2, y_lo: 2; y = y_hi * 2 + y_lo), z: 8, core: 2. Of those that a mesh axis runs over, the one named last changes fastest.
Arguments:
- tokens: bfloat16 [8, 256, 4096], P('section', None, ('expert', 'dp'))
- targets: bfloat16 [8, 256, 4096], P('section', None, ('expert', 'dp')), may hold values from -6 to 6
- group_ids: int32 [8, 256], P('section'), may hold values from 0 to 7, as said below
- expert_ids: int32 [1, 8, 8, 256, 2], P(None, 'section'), may hold values from 0 to 7, all different within a row; in each aligned block of 256 rows (0 to 255, 256 to 511, ..., all dimensions but the last counted through in order) at most 72 rows name the same one
- norm_gain: float32 [8, 4096], P('section', ('expert', 'dp')), may hold values from 0.5 to 1.5
- router: bfloat16 [8, 4096, 8], P('section', ('expert', 'dp')), may hold values from -0.09375 to 0.09375
- w_gate: bfloat16 [8, 8, 4096, 1536], P('section', 'expert', None, 'dp'), may hold values from -0.09375 to 0.09375
- w_up: bfloat16 [8, 8, 4096, 1536], P('section', 'expert', None, 'dp'), may hold values from -0.09375 to 0.09375
- w_down: bfloat16 [8, 8, 1536, 4096], P('section', 'expert', 'dp'), may hold values from -0.15625 to 0.15625
Outputs:
- grad_out: bfloat16 [8, 256, 4096], P('section', None, ('expert', 'dp'))
- group_loss: float32 [8], replicated
Inputs may be any that keep to these rules, and one draw needn't show every extreme that they name: `expert_ids`: in each aligned block of 256 rows (one micro-batch at one layer pass) no expert is named by more than 72 rows; a row names 2 different experts. `group_ids`: exactly one group has no rows; which one varies.
All inputs are finite; a program needn't handle non-finite values.
Results may differ from a plain program's by a relative error of at most 0.019.
Values may be sent and summed in bfloat16 or wider, within the bound.
A program may use at most 64 MiB of HBM per device.

v0:
```python
import jax
import jax.numpy as jnp
from jax import lax
from jax.sharding import PartitionSpec as P

GROUPS = 8


dro_rate = 0.3


def from_behind(value, axis, steps):
    count = lax.axis_size(axis)
    pairs = [(source, (source + steps) % count) for source in range(count)]
    return lax.ppermute(value, axis, pairs)


def per_device(tokens, targets, group_ids, expert_ids, norm_gain, router, w_gate, w_up, w_down):
    sections = lax.axis_size("section")
    lane_count = lax.axis_size("dp")
    experts = lax.axis_size("expert")
    circuits = expert_ids.shape[0]
    top_count = expert_ids.shape[-1]
    row_count = tokens.shape[1]
    piece_width = tokens.shape[2]
    full_width = piece_width * experts * lane_count
    capacity = min(row_count, row_count * top_count // experts * 9 // 8)
    section_place = lax.axis_index("section")
    gain_row = norm_gain[0]
    router_block = router[0]
    gate_matrix = w_gate[0, 0]
    up_matrix = w_up[0, 0]
    down_matrix = w_down[0, 0]
    expert_range = jnp.arange(experts, dtype=jnp.int32)
    slot_range = jnp.arange(capacity, dtype=jnp.int32)
    zero_index = jnp.zeros((), jnp.int32)

    def expert_rows(flat_rows):
        gate_part = jnp.dot(flat_rows, gate_matrix, preferred_element_type=jnp.float32)
        up_part = jnp.dot(flat_rows, up_matrix, preferred_element_type=jnp.float32)
        activated = (jax.nn.silu(gate_part) * up_part).astype(jnp.bfloat16)
        return jnp.dot(activated, down_matrix, preferred_element_type=jnp.float32).astype(
            jnp.bfloat16
        )

    def joined_work(received):
        item_count = received.shape[1]
        expert_part = expert_rows(received.reshape(item_count, full_width))
        return lax.all_to_all(
            expert_part.reshape(item_count, experts * lane_count, piece_width),
            ("expert", "dp"),
            split_axis=1,
            concat_axis=1,
            tiled=True,
        )

    def one_tick(moment, current):
        micro_index = (section_place - moment) % sections
        circuit = (moment // sections).astype(jnp.int32)
        choices = lax.dynamic_slice(
            expert_ids,
            (circuit, zero_index, micro_index, zero_index, zero_index),
            (1, 1, 1, row_count, top_count),
        ).reshape(row_count, top_count)
        wide_state = current.astype(jnp.float32)
        local_squares = jnp.sum(wide_state * wide_state, axis=1)
        total_squares = lax.psum(local_squares, ("expert", "dp"))
        row_scale = lax.rsqrt(total_squares / full_width + 1e-06)[:, None]
        normed = (wide_state * row_scale * gain_row[None, :]).astype(jnp.bfloat16)
        partial_logits = jnp.dot(normed, router_block, preferred_element_type=jnp.float32)
        logits = lax.psum(partial_logits, ("expert", "dp"))
        member = (choices[:, :, None] == expert_range[None, None, :]).astype(jnp.int32)
        flat_member = member.reshape(-1, experts)
        rank_before = jnp.cumsum(flat_member, axis=0) - flat_member
        position = jnp.sum(rank_before * flat_member, axis=1).reshape(row_count, top_count)
        chosen = jnp.sum(logits[:, None, :] * member.astype(jnp.float32), axis=2)
        weights = jnp.exp(chosen)
        gate_weights = weights / jnp.sum(weights, axis=1, keepdims=True)
        placement = member.astype(jnp.float32)[:, :, :, None] * (
            position[:, :, None, None] == slot_range[None, None, None, :]
        ).astype(jnp.float32)
        picker = (
            jnp.sum(placement, axis=1).reshape(row_count, experts * capacity).astype(jnp.bfloat16)
        )
        combiner = jnp.sum(placement * gate_weights[:, :, None, None], axis=1)
        outgoing = jnp.einsum(
            "us,ud->sd", picker, normed, preferred_element_type=jnp.float32
        ).astype(jnp.bfloat16)
        spread = jnp.broadcast_to(
            outgoing.reshape(experts, 1, capacity, piece_width),
            (experts, lane_count, capacity, piece_width),
        )
        returned = joined_work(
            lax.all_to_all(
                spread.reshape(experts * lane_count, capacity, piece_width),
                ("expert", "dp"),
                split_axis=0,
                concat_axis=2,
                tiled=True,
            )
        )
        lane_total = jnp.sum(
            returned.reshape(capacity, experts, lane_count, piece_width).astype(jnp.float32), axis=2
        )
        mixture = jnp.einsum("uec,ced->ud", combiner, lane_total, precision=lax.Precision.HIGHEST)
        updated = (wide_state + mixture).astype(jnp.bfloat16)
        return from_behind(updated, "section", 1)

    final_state = lax.fori_loop(0, circuits * sections, one_tick, tokens[0])
    difference = final_state.astype(jnp.float32) - targets[0].astype(jnp.float32)
    partial_squares = jnp.sum(difference * difference, axis=1) / full_width
    group_member = (group_ids[0][:, None] == jnp.arange(GROUPS, dtype=jnp.int32)[None, :]).astype(
        jnp.float32
    )
    local_totals = jnp.dot(partial_squares, group_member, precision=lax.Precision.HIGHEST)
    first_lane = ((lax.axis_index("expert") == 0) & (lax.axis_index("dp") == 0)).astype(jnp.float32)
    local_counts = jnp.sum(group_member, axis=0) * first_lane
    totals, counts = lax.psum((local_totals, local_counts), ("section", "expert", "dp"))
    group_loss = totals / jnp.maximum(counts, 1.0)
    raised = jnp.exp(dro_rate * group_loss)
    group_weight = raised / jnp.sum(raised)
    token_count = sections * row_count
    row_weight_table = group_weight * token_count / jnp.maximum(counts, 1.0)
    row_weight = jnp.dot(group_member, row_weight_table, precision=lax.Precision.HIGHEST)
    grad_out = (row_weight[:, None] * difference).astype(jnp.bfloat16)[None]
    return (grad_out, group_loss)


def solution(mesh):
    placed = (
        P("section", None, ("expert", "dp")),
        P("section", None, ("expert", "dp")),
        P("section", None),
        P(None, "section", None, None, None),
        P("section", ("expert", "dp")),
        P("section", ("expert", "dp"), None),
        P("section", "expert", None, "dp"),
        P("section", "expert", None, "dp"),
        P("section", "expert", "dp", None),
    )
    return jax.shard_map(
        per_device,
        mesh=mesh,
        in_specs=placed,
        out_specs=(P("section", None, ("expert", "dp")), P()),
        check_vma=False,
    )
```

profile of v0, /device:TPU:1, one launch (start us, length us, event | category | flops | bytes accessed | tf_op | source)
XLA Modules:
  0.0 1500.4 jit_solution(1334823001441641367)
XLA Ops:
  2.3 1422.9 %while.17 = (s32[]{:T(128)}, bf16[256,128]{1,0:T(8,128)(2,1)S(1)}, s32[]{:T(128)}, s32[1,1,8,256,2]{3,4,2,1,0:T(2,128)}, f32[1,128]{1,0:T(1,128)}, /*index=5*/bf...) while((s32[]{:T(128)}, bf16[256,128]{1,0:T(8,128)(2,1)S(1)}, ...), condition=%wide.region_12.13_spmd.clone.clone, body=%wide.region_0.12_spmd.clone.clone.sunk | while | flops 947298688 | bytes 33643788 | solution.py:109
  4.3 65.3 %psum.50 = f32[256]{0:T(256)S(1)} all-reduce(f32[256]{0:T(256)S(1)} %fusion.92), channel_id=1, replica_groups=mesh['section'=8,'expert'=8,'dp'=4] {'expert','dp'}, use_global_device_ids=true, to_apply=%region_5.5 | all-reduce | flops 256 | bytes 2048 | tf_op jit(solution)/shard_map/while/body/eval_jaxpr/psum | solution.py:67
  70.4 66.5 %psum.51 = f32[256,8]{0,1:T(8,128)S(1)} all-reduce(f32[256,8]{0,1:T(8,128)S(1)} %fusion.93), channel_id=1, replica_groups=mesh['section'=8,'expert'=8,'dp'=4] {'expert','dp'}, use_global_device_ids=true, to_apply=%region_6.6 | all-reduce | flops 2048 | bytes 16384 | tf_op jit(solution)/shard_map/while/body/eval_jaxpr/psum | solution.py:71
  161.6 16.2 %all_to_all.59 = bf16[72,32,128]{2,0,1:T(8,128)(2,1)S(1)} all-to-all(bf16[72,32,128]{2,0,1:T(8,128)(2,1)S(1)} %bitcast.119), channel_id=1, replica_groups=mesh['section'=8,'expert'=8,'dp'=4] {'expert','dp'}, dimensions={1} | all-to-all | bytes 1179648 | tf_op jit(solution)/shard_map/while/body/eval_jaxpr/all_to_all | solution.py:49
  188.4 63.6 %psum.50 = f32[256]{0:T(256)S(1)} all-reduce(f32[256]{0:T(256)S(1)} %fusion.92), channel_id=1, replica_groups=mesh['section'=8,'expert'=8,'dp'=4] {'expert','dp'}, use_global_device_ids=true, to_apply=%region_5.5 | all-reduce | flops 256 | bytes 2048 | tf_op jit(solution)/shard_map/while/body/eval_jaxpr/psum | solution.py:67
  253.0 63.6 %psum.51 = f32[256,8]{0,1:T(8,128)S(1)} all-reduce(f32[256,8]{0,1:T(8,128)S(1)} %fusion.93), channel_id=1, replica_groups=mesh['section'=8,'expert'=8,'dp'=4] {'expert','dp'}, use_global_device_ids=true, to_apply=%region_6.6 | all-reduce | flops 2048 | bytes 16384 | tf_op jit(solution)/shard_map/while/body/eval_jaxpr/psum | solution.py:71
  365.1 63.9 %psum.50 = f32[256]{0:T(256)S(1)} all-reduce(f32[256]{0:T(256)S(1)} %fusion.92), channel_id=1, replica_groups=mesh['section'=8,'expert'=8,'dp'=4] {'expert','dp'}, use_global_device_ids=true, to_apply=%region_5.5 | all-reduce | flops 256 | bytes 2048 | tf_op jit(solution)/shard_map/while/body/eval_jaxpr/psum | solution.py:67
  430.0 63.6 %psum.51 = f32[256,8]{0,1:T(8,128)S(1)} all-reduce(f32[256,8]{0,1:T(8,128)S(1)} %fusion.93), channel_id=1, replica_groups=mesh['section'=8,'expert'=8,'dp'=4] {'expert','dp'}, use_global_device_ids=true, to_apply=%region_6.6 | all-reduce | flops 2048 | bytes 16384 | tf_op jit(solution)/shard_map/while/body/eval_jaxpr/psum | solution.py:71
  518.2 16.2 %all_to_all.59 = bf16[72,32,128]{2,0,1:T(8,128)(2,1)S(1)} all-to-all(bf16[72,32,128]{2,0,1:T(8,128)(2,1)S(1)} %bitcast.119), channel_id=1, replica_groups=mesh['section'=8,'expert'=8,'dp'=4] {'expert','dp'}, dimensions={1} | all-to-all | bytes 1179648 | tf_op jit(solution)/shard_map/while/body/eval_jaxpr/all_to_all | solution.py:49
  542.1 63.9 %psum.50 = f32[256]{0:T(256)S(1)} all-reduce(f32[256]{0:T(256)S(1)} %fusion.92), channel_id=1, replica_groups=mesh['section'=8,'expert'=8,'dp'=4] {'expert','dp'}, use_global_device_ids=true, to_apply=%region_5.5 | all-reduce | flops 256 | bytes 2048 | tf_op jit(solution)/shard_map/while/body/eval_jaxpr/psum | solution.py:67
  607.0 63.6 %psum.51 = f32[256,8]{0,1:T(8,128)S(1)} all-reduce(f32[256,8]{0,1:T(8,128)S(1)} %fusion.93), channel_id=1, replica_groups=mesh['section'=8,'expert'=8,'dp'=4] {'expert','dp'}, use_global_device_ids=true, to_apply=%region_6.6 | all-reduce | flops 2048 | bytes 16384 | tf_op jit(solution)/shard_map/while/body/eval_jaxpr/psum | solution.py:71
  719.1 63.9 %psum.50 = f32[256]{0:T(256)S(1)} all-reduce(f32[256]{0:T(256)S(1)} %fusion.92), channel_id=1, replica_groups=mesh['section'=8,'expert'=8,'dp'=4] {'expert','dp'}, use_global_device_ids=true, to_apply=%region_5.5 | all-reduce | flops 256 | bytes 2048 | tf_op jit(solution)/shard_map/while/body/eval_jaxpr/psum | solution.py:67
  784.0 63.6 %psum.51 = f32[256,8]{0,1:T(8,128)S(1)} all-reduce(f32[256,8]{0,1:T(8,128)S(1)} %fusion.93), channel_id=1, replica_groups=mesh['section'=8,'expert'=8,'dp'=4] {'expert','dp'}, use_global_device_ids=true, to_apply=%region_6.6 | all-reduce | flops 2048 | bytes 16384 | tf_op jit(solution)/shard_map/while/body/eval_jaxpr/psum | solution.py:71
  872.2 16.2 %all_to_all.59 = bf16[72,32,128]{2,0,1:T(8,128)(2,1)S(1)} all-to-all(bf16[72,32,128]{2,0,1:T(8,128)(2,1)S(1)} %bitcast.119), channel_id=1, replica_groups=mesh['section'=8,'expert'=8,'dp'=4] {'expert','dp'}, dimensions={1} | all-to-all | bytes 1179648 | tf_op jit(solution)/shard_map/while/body/eval_jaxpr/all_to_all | solution.py:49
  896.1 63.9 %psum.50 = f32[256]{0:T(256)S(1)} all-reduce(f32[256]{0:T(256)S(1)} %fusion.92), channel_id=1, replica_groups=mesh['section'=8,'expert'=8,'dp'=4] {'expert','dp'}, use_global_device_ids=true, to_apply=%region_5.5 | all-reduce | flops 256 | bytes 2048 | tf_op jit(solution)/shard_map/while/body/eval_jaxpr/psum | solution.py:67
  960.9 63.6 %psum.51 = f32[256,8]{0,1:T(8,128)S(1)} all-reduce(f32[256,8]{0,1:T(8,128)S(1)} %fusion.93), channel_id=1, replica_groups=mesh['section'=8,'expert'=8,'dp'=4] {'expert','dp'}, use_global_device_ids=true, to_apply=%region_6.6 | all-reduce | flops 2048 | bytes 16384 | tf_op jit(solution)/shard_map/while/body/eval_jaxpr/psum | solution.py:71
  1049.2 16.2 %all_to_all.59 = bf16[72,32,128]{2,0,1:T(8,128)(2,1)S(1)} all-to-all(bf16[72,32,128]{2,0,1:T(8,128)(2,1)S(1)} %bitcast.119), channel_id=1, replica_groups=mesh['section'=8,'expert'=8,'dp'=4] {'expert','dp'}, dimensions={1} | all-to-all | bytes 1179648 | tf_op jit(solution)/shard_map/while/body/eval_jaxpr/all_to_all | solution.py:49
  1073.1 63.9 %psum.50 = f32[256]{0:T(256)S(1)} all-reduce(f32[256]{0:T(256)S(1)} %fusion.92), channel_id=1, replica_groups=mesh['section'=8,'expert'=8,'dp'=4] {'expert','dp'}, use_global_device_ids=true, to_apply=%region_5.5 | all-reduce | flops 256 | bytes 2048 | tf_op jit(solution)/shard_map/while/body/eval_jaxpr/psum | solution.py:67
  1137.9 63.6 %psum.51 = f32[256,8]{0,1:T(8,128)S(1)} all-reduce(f32[256,8]{0,1:T(8,128)S(1)} %fusion.93), channel_id=1, replica_groups=mesh['section'=8,'expert'=8,'dp'=4] {'expert','dp'}, use_global_device_ids=true, to_apply=%region_6.6 | all-reduce | flops 2048 | bytes 16384 | tf_op jit(solution)/shard_map/while/body/eval_jaxpr/psum | solution.py:71
  1226.2 16.2 %all_to_all.59 = bf16[72,32,128]{2,0,1:T(8,128)(2,1)S(1)} all-to-all(bf16[72,32,128]{2,0,1:T(8,128)(2,1)S(1)} %bitcast.119), channel_id=1, replica_groups=mesh['section'=8,'expert'=8,'dp'=4] {'expert','dp'}, dimensions={1} | all-to-all | bytes 1179648 | tf_op jit(solution)/shard_map/while/body/eval_jaxpr/all_to_all | solution.py:49
  1250.1 63.9 %psum.50 = f32[256]{0:T(256)S(1)} all-reduce(f32[256]{0:T(256)S(1)} %fusion.92), channel_id=1, replica_groups=mesh['section'=8,'expert'=8,'dp'=4] {'expert','dp'}, use_global_device_ids=true, to_apply=%region_5.5 | all-reduce | flops 256 | bytes 2048 | tf_op jit(solution)/shard_map/while/body/eval_jaxpr/psum | solution.py:67
  1314.9 63.6 %psum.51 = f32[256,8]{0,1:T(8,128)S(1)} all-reduce(f32[256,8]{0,1:T(8,128)S(1)} %fusion.93), channel_id=1, replica_groups=mesh['section'=8,'expert'=8,'dp'=4] {'expert','dp'}, use_global_device_ids=true, to_apply=%region_6.6 | all-reduce | flops 2048 | bytes 16384 | tf_op jit(solution)/shard_map/while/body/eval_jaxpr/psum | solution.py:71
  1403.2 16.2 %all_to_all.59 = bf16[72,32,128]{2,0,1:T(8,128)(2,1)S(1)} all-to-all(bf16[72,32,128]{2,0,1:T(8,128)(2,1)S(1)} %bitcast.119), channel_id=1, replica_groups=mesh['section'=8,'expert'=8,'dp'=4] {'expert','dp'}, dimensions={1} | all-to-all | bytes 1179648 | tf_op jit(solution)/shard_map/while/body/eval_jaxpr/all_to_all | solution.py:49
  1425.4 72.8 %all-reduce = (f32[8]{0:T(128)S(1)}, f32[8]{0:T(128)S(1)}) all-reduce(f32[8]{0:T(128)S(1)} %broadcast_multiply_fusion.1, f32[8]{0:T(128)S(1)} %convolution_bitcast_fusion.1), channel_id=1, replica_groups=mesh['section'=8,'expert'=8,'dp'=4] {'section','expert','dp'}, use_global_device_ids=true, to_apply=%region_16.17 | all-reduce | flops 16 | bytes 128 | tf_op jit(solution)/shard_map/psum | solution.py:118
  (297 shorter events, 303.8 us)
Async XLA Ops:
  2.3 1422.9 %copy-start.1 = (bf16[1,256,128]{2,1,0:T(8,128)(2,1)S(1)}, bf16[1,256,128]{2,1,0:T(8,128)(2,1)}, u32[]{:S(2)}) copy-start(bf16[1,256,128]{2,1,0:T(8,128)(2,1)} %param.12) | copy-start | bytes 196612
  2.3 1423.0 %copy-start.3 = (s32[1,256]{1,0:T(1,128)S(1)}, s32[1,256]{1,0:T(1,128)}, u32[]{:S(2)}) copy-start(s32[1,256]{1,0:T(1,128)} %param.13) | copy-start | bytes 3076
  138.8 17.4 %copy-start = (bf16[4096,384]{1,0:T(8,128)(2,1)S(1)}, bf16[4096,384]{1,0:T(8,128)(2,1)}, u32[]{:S(2)}) copy-start(bf16[4096,384]{1,0:T(8,128)(2,1)} %get-tuple-element.482) | copy-start | bytes 9437188 | tf_op jit(solution)/shard_map/while
  179.2 7.3 collective-permute-start
  318.4 17.4 %copy-start = (bf16[4096,384]{1,0:T(8,128)(2,1)S(1)}, bf16[4096,384]{1,0:T(8,128)(2,1)}, u32[]{:S(2)}) copy-start(bf16[4096,384]{1,0:T(8,128)(2,1)} %get-tuple-element.482) | copy-start | bytes 9437188 | tf_op jit(solution)/shard_map/while
  358.8 4.4 collective-permute-start
  495.4 17.4 %copy-start = (bf16[4096,384]{1,0:T(8,128)(2,1)S(1)}, bf16[4096,384]{1,0:T(8,128)(2,1)}, u32[]{:S(2)}) copy-start(bf16[4096,384]{1,0:T(8,128)(2,1)} %get-tuple-element.482) | copy-start | bytes 9437188 | tf_op jit(solution)/shard_map/while
  535.8 4.4 collective-permute-start
  672.4 17.4 %copy-start = (bf16[4096,384]{1,0:T(8,128)(2,1)S(1)}, bf16[4096,384]{1,0:T(8,128)(2,1)}, u32[]{:S(2)}) copy-start(bf16[4096,384]{1,0:T(8,128)(2,1)} %get-tuple-element.482) | copy-start | bytes 9437188 | tf_op jit(solution)/shard_map/while
  712.8 4.4 collective-permute-start
  849.4 17.4 %copy-start = (bf16[4096,384]{1,0:T(8,128)(2,1)S(1)}, bf16[4096,384]{1,0:T(8,128)(2,1)}, u32[]{:S(2)}) copy-start(bf16[4096,384]{1,0:T(8,128)(2,1)} %get-tuple-element.482) | copy-start | bytes 9437188 | tf_op jit(solution)/shard_map/while
  889.8 4.4 collective-permute-start
  1026.4 17.4 %copy-start = (bf16[4096,384]{1,0:T(8,128)(2,1)S(1)}, bf16[4096,384]{1,0:T(8,128)(2,1)}, u32[]{:S(2)}) copy-start(bf16[4096,384]{1,0:T(8,128)(2,1)} %get-tuple-element.482) | copy-start | bytes 9437188 | tf_op jit(solution)/shard_map/while
  1066.8 4.4 collective-permute-start
  1203.4 17.4 %copy-start = (bf16[4096,384]{1,0:T(8,128)(2,1)S(1)}, bf16[4096,384]{1,0:T(8,128)(2,1)}, u32[]{:S(2)}) copy-start(bf16[4096,384]{1,0:T(8,128)(2,1)} %get-tuple-element.482) | copy-start | bytes 9437188 | tf_op jit(solution)/shard_map/while
  1243.8 4.4 collective-permute-start
  1380.4 17.4 %copy-start = (bf16[4096,384]{1,0:T(8,128)(2,1)S(1)}, bf16[4096,384]{1,0:T(8,128)(2,1)}, u32[]{:S(2)}) copy-start(bf16[4096,384]{1,0:T(8,128)(2,1)} %get-tuple-element.482) | copy-start | bytes 9437188 | tf_op jit(solution)/shard_map/while
  1420.8 4.4 collective-permute-start
  1498.9 1.5 copy-start.2
where the time goes:
time: 1500 us
  blocking collectives  1350 us (90%)
  matrix products  68.6 us (5%)
  waiting for transfers between devices  35.8 us (2%)
  local copies, waits for them, and re-layouts  20.9 us (1%)
  other arithmetic  16.5 us (1%)
    psum x8, blocking collectives, one_tick(): total_squares = lax.psum(local_squares, ('expert', 'dp'))  512 us
    psum x8, blocking collectives, one_tick(): logits = lax.psum(partial_logits, ('expert', 'dp'))  512 us
    all_to_all x8, blocking collectives, joined_work(): lax.all_to_all(expert_part.reshape(item_count, experts * lane_count, piec...  130 us
    all_to_all x8, blocking collectives, one_tick(): lax.all_to_all(spread.reshape(experts * lane_count, capacity, piece_width...  127 us
    psum x1, blocking collectives, per_device(): lax.psum((local_totals, local_counts), ('section', 'expert', 'dp'))  72.8 us
    ppermute x8, waiting for transfers between devices, from_behind(): return lax.ppermute(value, axis, pairs)  35.8 us
    dot_general x8, matrix products, expert_rows(): jnp.dot(activated, down_matrix, preferred_element_type=jnp.float32)  35.4 us
  transfers between devices with their start and end apart: 8, of which 8 were waited for; matrix products, arithmetic and copies ran while one was open for 0% of the time, Pallas kernels for 0%

commit v1 on v0

v1 whole, which is shorter than its diff:
```python
import functools

import jax
import jax.numpy as jnp
from jax import lax
from jax.experimental import pallas as pl
from jax.experimental.pallas import tpu as pltpu
from jax.sharding import PartitionSpec as P

MESH = pl.DeviceIdType.MESH
GROUPS = 8
TOPK = 2
DRO_RATE = 0.3
LANES = 128
F32 = jnp.float32
BF16 = jnp.bfloat16
LAST_DIMS = (((1,), (1,)), ((), ()))


def dot(a, b):
    return jnp.dot(a, b, preferred_element_type=F32)


def dot_t(a, b):
    return lax.dot_general(a, b, LAST_DIMS, preferred_element_type=F32)


def ones_where(mask):
    return jnp.where(mask, 1.0, 0.0).astype(BF16)


def kernel(
    sections, experts, slots, per_group, width,
    tok_ref, tgt_ref, gid_ref, ids_ref, gain_ref, rt_ref, wg_ref, wu_ref, wd_ref,
    grad_ref, loss_ref,
    w_gu, w_dn, x_all, x_new, out_buf, x_in, acc, sq_acc, logit_acc, act, dn_acc, part_out, part_in,
    pick, scat, member, columns, upper, eye, rt_mine, rt_in, rt_bf, red_mine, red_in, red_sib, red_z,
    w_sem, wd_sem, wd_send, wd_recv, d_send, d_recv, f_send, f_recv, a_send, a_recv,
    c_send, c_recv, z_send, z_recv, r_send, r_recv, rf_send, rf_recv, s_send, s_recv,
    sb_send, sb_recv, sz_send, sz_recv,
):
    chips = experts * 2
    rows = tok_ref.shape[0]
    hidden = wg_ref.shape[-1]
    section = lax.axis_index("section")
    expert = lax.axis_index("expert")
    lane = lax.axis_index("dp")
    core = lax.rem(lane, 2)
    half = lane // 2
    mine = expert * 2 + half
    other = 1 - core
    sibling = (section, expert, half * 2 + other)

    def peer(step):
        place = lax.rem(mine + step, chips)
        return place, (section, place // 2, lax.rem(place, 2) * 2 + core)

    def source(step):
        return lax.rem(mine + chips - step, chips)

    def along_z(step):
        return (lax.rem(section + step, sections), expert, lane)

    def remote(src, dst, send, recv, device):
        return pltpu.make_async_remote_copy(
            src_ref=src, dst_ref=dst, send_sem=send, recv_sem=recv, device_id=device, device_id_type=MESH
        )

    loads = []
    for side in range(2):
        loads.append(pltpu.make_async_copy(wg_ref.at[:, side], w_gu.at[side, :, :, 0:hidden], w_sem.at[2 * side]))
        loads.append(
            pltpu.make_async_copy(wu_ref.at[:, side], w_gu.at[side, :, :, hidden : 2 * hidden], w_sem.at[2 * side + 1])
        )
    for j in range(chips):
        own_columns = pl.ds(pl.multiple_of(j * 2 * LANES + core * LANES, LANES), LANES)
        loads.append(pltpu.make_async_copy(wd_ref.at[:, own_columns], w_dn.at[core, j], wd_sem.at[j]))
    for load in loads:
        load.start()

    barrier = pltpu.get_barrier_semaphore()
    for step in range(1, chips):
        pl.semaphore_signal(barrier, inc=1, device_id=peer(step)[1], device_id_type=MESH)
    pl.semaphore_signal(barrier, inc=1, device_id=sibling, device_id_type=MESH)
    for step in range(1, sections):
        pl.semaphore_signal(barrier, inc=1, device_id=along_z(step), device_id_type=MESH)

    gain = gain_ref[...]
    rt_mine[0:8, :] = rt_ref[...]
    rt_mine[8:16, :] = jnp.broadcast_to(1.0 / (gain * gain), (8, LANES))
    rt_in[core, 0] = rt_mine[...]
    first = lax.broadcasted_iota(jnp.int32, (rows, rows), 0)
    second = lax.broadcasted_iota(jnp.int32, (rows, rows), 1)
    upper[...] = ones_where(first < second)
    eye[...] = ones_where(first == second)
    x_all[0] = tok_ref[...]

    expert_rows = lax.broadcasted_iota(jnp.int32, (16, rows), 0)

    def prepare_pick(moment):
        micro = lax.rem(section + 2 * sections - moment, sections)
        first_id = ids_ref[micro, 0:1, :]
        second_id = ids_ref[micro, 1:2, :]
        hit_first = first_id == expert_rows
        hit_second = second_id == expert_rows
        either = hit_first | hit_second
        named = ones_where(either)
        rank = dot(named, upper[...])
        member[...] = named
        rank_first = jnp.sum(jnp.where(hit_first, rank, 0.0), axis=0, keepdims=True)
        rank_second = jnp.sum(jnp.where(hit_second, rank, 0.0), axis=0, keepdims=True)
        table = jnp.where(expert_rows == 0, first_id.astype(F32), second_id.astype(F32))
        table = jnp.where(expert_rows == 2, rank_first, table)
        table = jnp.where(expert_rows == 3, rank_second, table)
        columns[...] = table.astype(BF16)
        key = jnp.where(either, rank, -1.0)
        slot_rows = lax.broadcasted_iota(jnp.int32, (slots, rows), 0).astype(F32)
        for e in range(experts):
            pick[e * slots : (e + 1) * slots, :] = ones_where(key[e : e + 1, :] == slot_rows)

    def prepare_scatter():
        spread = dot_t(eye[...], columns[...])
        slot_first = spread[:, 0:1] * slots + spread[:, 2:3]
        slot_second = spread[:, 1:2] * slots + spread[:, 3:4]
        lanes = lax.broadcasted_iota(jnp.int32, (rows, LANES), 1).astype(F32)
        for n in range(experts * slots // LANES):
            here = lanes + float(n * LANES)
            scat[:, n * LANES : (n + 1) * LANES] = ones_where((slot_first == here) | (slot_second == here))

    prepare_pick(0)

    pl.semaphore_wait(barrier, chips + sections - 1)

    for step in range(1, chips):
        remote(rt_mine, rt_in.at[core, step], r_send.at[step], r_recv.at[step], peer(step)[1]).start()
    for j in range(chips):
        sib_columns = pl.ds(pl.multiple_of(j * 2 * LANES + other * LANES, LANES), LANES)
        remote(wd_ref.at[:, sib_columns], w_dn.at[core, j], wd_send.at[j], wd_recv.at[j], sibling).start()

    def dispatch(moment):
        scaled = (x_all[moment].astype(F32) * gain).astype(BF16)
        out_buf[...] = dot(pick[...], scaled).astype(BF16)
        for step in range(1, chips):
            place, device = peer(step)
            block = pl.ds(pl.multiple_of((place // 2) * slots, 16), slots)
            remote(out_buf.at[block, :], x_in.at[core, step], d_send.at[step], d_recv.at[step], device).start()
        own_block = pl.ds(pl.multiple_of(expert * slots, 16), slots)
        x_in[core, 0] = out_buf[own_block, :]

    def router_blocks():
        for step in range(1, chips):
            copy = remote(rt_mine, rt_in.at[core, step], r_send.at[step], r_recv.at[step], peer(step)[1])
            copy.wait_recv()
            copy.wait_send()
        forward = remote(rt_in.at[core], rt_in.at[core], rf_send.at[0], rf_recv.at[0], sibling)
        forward.start()
        forward.wait_send()
        remote(rt_in.at[other], rt_in.at[other], rf_send.at[0], rf_recv.at[0], sibling).wait_recv()
        for side in range(2):
            for step in range(chips):
                rt_bf[side, :, step * LANES : (step + 1) * LANES] = rt_in[side, step].astype(BF16)

    def weights_here():
        for load in loads:
            load.wait()
        for j in range(chips):
            copy = remote(
                wd_ref.at[:, pl.ds(0, LANES)], w_dn.at[other, j], wd_send.at[j], wd_recv.at[j], sibling
            )
            copy.wait_send()
            copy.wait_recv()

    group_count = chips // per_group

    def group_work(side, g, fresh):
        steps = range(g * per_group, (g + 1) * per_group)
        blocks = [x_in[side, step] for step in steps]
        block = jnp.concatenate(blocks, axis=1)
        weight = jnp.concatenate([w_gu[side, source(step)] for step in steps], axis=0)
        product = dot(block, weight)
        router = rt_bf[side, :, g * per_group * LANES : (g + 1) * per_group * LANES]
        logits = dot_t(block, router)
        squares = None
        for step, piece in zip(steps, blocks):
            wide = piece.astype(F32)
            term = wide * wide * rt_in[side, step, 8:9, :]
            squares = term if squares is None else squares + term
        if fresh:
            acc[...] = product
            logit_acc[...] = logits
            sq_acc[...] = squares
        else:
            acc[...] += product
            logit_acc[...] += logits
            sq_acc[...] += squares

    def own_group(g, fresh=False):
        for step in range(max(1, g * per_group), (g + 1) * per_group):
            remote(
                out_buf.at[pl.ds(0, slots), :], x_in.at[core, step], d_send.at[step], d_recv.at[step], sibling
            ).wait_recv()
        block = pl.ds(g * per_group, per_group)
        remote(x_in.at[core, block], x_in.at[core, block], f_send.at[g], f_recv.at[g], sibling).start()
        group_work(core, g, fresh)

    def sibling_group(g):
        block = pl.ds(g * per_group, per_group)
        remote(x_in.at[other, block], x_in.at[other, block], f_send.at[g], f_recv.at[g], sibling).wait_recv()
        group_work(other, g, False)

    def tick(moment, carry):
        dispatch(moment)
        prepare_scatter()

        @pl.when(moment == 0)
        def _():
            router_blocks()
            weights_here()

        own_group(0, True)
        for g in range(1, group_count):
            own_group(g)
            sibling_group(g - 1)
        sibling_group(group_count - 1)

        row_scale = lax.rsqrt(jnp.sum(sq_acc[...], axis=1, keepdims=True) / width + 1e-6)
        gate_part = acc[:, 0:hidden] * row_scale
        up_part = acc[:, hidden : 2 * hidden] * row_scale
        act[core] = (gate_part / (1.0 + jnp.exp(-gate_part)) * up_part).astype(BF16)
        swap = remote(act.at[core], act.at[core], a_send.at[0], a_recv.at[0], sibling)
        swap.start()

        own_pick = pick[pl.ds(pl.multiple_of(expert * slots, 16), slots), :]
        chosen = dot_t(own_pick, member[...]) > 0.5
        logits = logit_acc[...] * row_scale
        lanes = lax.broadcasted_iota(jnp.int32, (slots, 16), 1)
        top = jnp.max(jnp.where(chosen, logits, -1e30), axis=1, keepdims=True)
        raised = jnp.where(chosen, jnp.exp(jnp.where(chosen, logits - top, 0.0)), 0.0)
        gate = jnp.sum(jnp.where(lanes == expert, raised, 0.0), axis=1, keepdims=True) / jnp.maximum(
            jnp.sum(raised, axis=1, keepdims=True), 1e-30
        )

        orders = [(step, (step + 1) % chips) for step in range(1, chips, 2)]

        def down_weight(side, pair):
            return jnp.concatenate([w_dn[side, lax.rem(mine + step, chips)] for step in pair], axis=1)

        own_act = act[core]
        for i, pair in enumerate(orders):
            dn_acc[i] = dot(own_act, down_weight(core, pair))
        for g in range(group_count):
            block = pl.ds(g * per_group, per_group)
            remote(x_in.at[core, block], x_in.at[core, block], f_send.at[g], f_recv.at[g], sibling).wait_send()
        for step in range(1, chips):
            remote(
                out_buf.at[pl.ds(0, slots), :], x_in.at[core, step], d_send.at[step], d_recv.at[step], sibling
            ).wait_send()
        remote(act.at[other], act.at[other], a_send.at[0], a_recv.at[0], sibling).wait_recv()
        swap.wait_send()
        sib_act = act[other]
        landing = pl.ds(pl.multiple_of((half * experts + expert) * slots, 16), slots)
        for i, pair in enumerate(orders):
            piece = ((dn_acc[i] + dot(sib_act, down_weight(other, pair))) * gate).astype(BF16)
            for at, step in enumerate(pair):
                value = piece[:, at * LANES : (at + 1) * LANES]
                if step == 0:
                    part_in[landing, :] = value
                else:
                    part_out[step] = value
                    remote(
                        part_out.at[step], part_in.at[landing, :], c_send.at[step], c_recv.at[step], peer(step)[1]
                    ).start()

        prepare_pick(moment + 1)

        for step in range(1, chips):
            copy = remote(
                part_out.at[step], part_in.at[pl.ds(0, slots), :], c_send.at[step], c_recv.at[step], sibling
            )
            copy.wait_recv()
            copy.wait_send()
        table = scat[...]
        count = experts * slots
        moe = dot(table, part_in[0:count, :]) + dot(table, part_in[count : 2 * count, :])
        x_new[...] = (x_all[moment].astype(F32) + moe).astype(BF16)
        onward = remote(x_new, x_all.at[moment + 1], z_send.at[0], z_recv.at[moment], along_z(1))
        onward.start()
        onward.wait_send()
        onward.wait_recv()
        return carry

    lax.fori_loop(0, sections, tick, 0)

    difference = x_all[sections].astype(F32) - tgt_ref[...].astype(F32)
    row_loss = jnp.sum(difference * difference, axis=1, keepdims=True) / width
    group_row = gid_ref[...]
    group_column = dot_t(eye[...], jnp.broadcast_to(group_row.astype(F32), (16, rows)).astype(BF16))[:, 0:1]
    lanes = lax.broadcasted_iota(jnp.int32, (rows, LANES), 1).astype(F32)
    belongs = jnp.where(group_column == lanes, 1.0, 0.0)
    totals = jnp.sum(belongs * row_loss, axis=0, keepdims=True)
    counts = jnp.sum(belongs, axis=0, keepdims=True)
    red_rows = lax.broadcasted_iota(jnp.int32, (8, LANES), 0)
    local = jnp.where(red_rows == 0, totals, counts)
    red_mine[0] = local
    red_in[mine] = local
    for step in range(1, chips):
        remote(red_mine.at[0], red_in.at[mine], s_send.at[step], s_recv.at[step], peer(step)[1]).start()
    for step in range(1, chips):
        copy = remote(red_mine.at[0], red_in.at[source(step)], s_send.at[step], s_recv.at[step], peer(step)[1])
        copy.wait_recv()
        copy.wait_send()
    plane = red_in[0]
    for j in range(1, chips):
        plane = plane + red_in[j]
    red_mine[1] = plane
    across = remote(red_mine.at[1], red_sib, sb_send.at[0], sb_recv.at[0], sibling)
    across.start()
    across.wait_send()
    across.wait_recv()
    both = plane + red_sib[...]
    red_mine[2] = both
    red_z[section] = both
    for step in range(1, sections):
        remote(red_mine.at[2], red_z.at[section], sz_send.at[step], sz_recv.at[step], along_z(step)).start()
    for step in range(1, sections):
        there = lax.rem(section + sections - step, sections)
        copy = remote(red_mine.at[2], red_z.at[there], sz_send.at[step], sz_recv.at[step], along_z(step))
        copy.wait_recv()
        copy.wait_send()
    whole = red_z[0]
    for j in range(1, sections):
        whole = whole + red_z[j]
    total = whole[0:1, :]
    count = whole[1:2, :] / (chips * 2)
    safe = jnp.maximum(count, 1.0)
    group_loss = total / safe
    lane_row = lax.broadcasted_iota(jnp.int32, (1, LANES), 1)
    raised = jnp.where(lane_row < GROUPS, jnp.exp(DRO_RATE * group_loss), 0.0)
    weight = raised / jnp.sum(raised, axis=1, keepdims=True) * (sections * rows) / safe
    row_weight = jnp.sum(belongs * weight, axis=1, keepdims=True)
    grad_ref[...] = (row_weight * difference).astype(BF16)
    loss_ref[...] = jnp.broadcast_to(group_loss, (8, LANES))


def per_device(slots, per_group, tokens, targets, group_ids, expert_ids, norm_gain, router, w_gate, w_up, w_down):
    sections = lax.axis_size("section")
    experts = lax.axis_size("expert")
    chips = experts * 2
    rows = tokens.shape[1]
    width = w_gate.shape[2]
    hidden = w_gate.shape[3]
    ids = jnp.transpose(expert_ids[0, 0], (0, 2, 1))
    router_rows = jnp.zeros((8, LANES), F32).at[:experts].set(jnp.transpose(router[0].astype(F32)))
    vmem = pl.BlockSpec(memory_space=pltpu.VMEM)
    anywhere = pl.BlockSpec(memory_space=pl.ANY)
    dma = pltpu.SemaphoreType.DMA
    scratch = [
        pltpu.VMEM((2, chips, LANES, 2 * hidden), BF16),
        pltpu.VMEM((2, chips, hidden, LANES), BF16),
        pltpu.VMEM((sections + 1, rows, LANES), BF16),
        pltpu.VMEM((rows, LANES), BF16),
        pltpu.VMEM((experts * slots, LANES), BF16),
        pltpu.VMEM((2, chips, slots, LANES), BF16),
        pltpu.VMEM((slots, 2 * hidden), F32),
        pltpu.VMEM((slots, LANES), F32),
        pltpu.VMEM((slots, 16), F32),
        pltpu.VMEM((2, slots, hidden), BF16),
        pltpu.VMEM((chips // 2, slots, 2 * LANES), F32),
        pltpu.VMEM((chips, slots, LANES), BF16),
        pltpu.VMEM((chips * slots, LANES), BF16),
        pltpu.VMEM((experts * slots, rows), BF16),
        pltpu.VMEM((rows, experts * slots), BF16),
        pltpu.VMEM((16, rows), BF16),
        pltpu.VMEM((16, rows), BF16),
        pltpu.VMEM((rows, rows), BF16),
        pltpu.VMEM((rows, rows), BF16),
        pltpu.VMEM((16, LANES), F32),
        pltpu.VMEM((2, chips, 16, LANES), F32),
        pltpu.VMEM((2, 16, chips * LANES), BF16),
        pltpu.VMEM((3, 8, LANES), F32),
        pltpu.VMEM((chips, 8, LANES), F32),
        pltpu.VMEM((8, LANES), F32),
        pltpu.VMEM((sections, 8, LANES), F32),
        dma((4,)),
        dma((chips,)),
        dma((chips,)),
        dma((chips,)),
        dma((chips,)),
        dma((chips,)),
        dma((chips // per_group,)),
        dma((chips // per_group,)),
        dma((1,)),
        dma((1,)),
        dma((chips,)),
        dma((chips,)),
        dma((1,)),
        dma((sections,)),
        dma((chips,)),
        dma((chips,)),
        dma((1,)),
        dma((1,)),
        dma((chips,)),
        dma((chips,)),
        dma((1,)),
        dma((1,)),
        dma((sections,)),
        dma((sections,)),
    ]
    grad, loss = pl.pallas_call(
        functools.partial(kernel, sections, experts, slots, per_group, float(width)),
        out_shape=(
            jax.ShapeDtypeStruct((rows, LANES), BF16),
            jax.ShapeDtypeStruct((8, LANES), F32),
        ),
        in_specs=[vmem] * 6 + [anywhere] * 3,
        out_specs=(vmem, vmem),
        scratch_shapes=scratch,
        compiler_params=pltpu.CompilerParams(
            collective_id=0, has_side_effects=True, vmem_limit_bytes=60 * 1024 * 1024
        ),
        name="moe_ring",
    )(
        tokens[0],
        targets[0],
        group_ids,
        ids,
        norm_gain,
        router_rows,
        w_gate.reshape(chips, 2, LANES, hidden),
        w_up.reshape(chips, 2, LANES, hidden),
        w_down.reshape(hidden, width),
    )
    return grad[None], loss[0, :GROUPS]


def build(mesh, slots, per_group):
    placed = (
        P("section", None, ("expert", "dp")),
        P("section", None, ("expert", "dp")),
        P("section", None),
        P(None, "section", None, None, None),
        P("section", ("expert", "dp")),
        P("section", ("expert", "dp"), None),
        P("section", "expert", None, "dp"),
        P("section", "expert", None, "dp"),
        P("section", "expert", "dp", None),
    )
    return jax.shard_map(
        functools.partial(per_device, slots, per_group),
        mesh=mesh,
        in_specs=placed,
        out_specs=(P("section", None, ("expert", "dp")), P()),
        check_vma=False,
    )


def solution(mesh):
    return build(mesh, 80, 4)
```

time: 1500 us -> 201 us (0.13)
  blocking collectives: 1350 us -> 0 us
  Pallas kernels: 0 us -> 196 us
  matrix products: 68.6 us -> 0 us
  waiting for transfers between devices: 35.8 us -> 0 us
  local copies, waits for them, and re-layouts: 20.9 us -> 2.66 us
  other arithmetic: 16.5 us -> 1.28 us
    psum x17 -> x0, blocking collectives: 1100 us -> none  [the longest x8 512 us: one_tick(): total_squares = lax.psum(local_squares, ('expert', 'dp'))]
    all_to_all x16 -> x0, blocking collectives: 257 us -> none  [the longest x8 130 us: joined_work(): lax.all_to_all(expert_part.reshape(item_count, experts * lane_count, piec...]
    pallas_call x0 -> x1, Pallas kernels: none -> 196 us  [per_device(): pl.pallas_call(functools.partial(kernel, sections, experts, slots, per_gr...]
    dot_general x42 -> x0, matrix products: 68.6 us -> none  [the longest x8 35.4 us: expert_rows(): jnp.dot(activated, down_matrix, preferred_element_type=jnp.float32)]
    ppermute x8 -> x0, waiting for transfers between devices: 35.8 us -> none  [from_behind(): return lax.ppermute(value, axis, pairs)]
  transfers between devices with their start and end apart: 8 -> 0, of which waited for: 8 -> 0; matrix products, arithmetic and copies ran while one was open for 0% -> 0% of each run, Pallas kernels for 0% -> 0%
where the time goes in v1:
time: 201 us
  Pallas kernels  196 us (98%)
  local copies, waits for them, and re-layouts  2.66 us (1%)
    pallas_call x1, Pallas kernels, per_device(): pl.pallas_call(functools.partial(kernel, sections, experts, slots, per_gr...  196 us

profile of v1, /device:TPU:1, one launch (start us, length us, event | category | flops | bytes accessed | tf_op | source)
XLA Modules:
  0.0 200.5 jit_solution(8507405279762477593)
XLA Ops:
  0.6 1.3 convert_bitcast_fusion.rt_ref
  1.9 196.0 %moe_ring.1 = (bf16[256,128]{1,0:T(8,128)(2,1)}, f32[8,128]{1,0:T(8,128)}) custom-call(bf16[256,128]{1,0:T(8,128)(2,1)} %bitcast.19, bf16[256,128]{1,0:T(8,128)(2,1)} %bitcast.20, s32[1,256]{1,0:T(1,128)} %gid_ref.1, s32[8,2,256]{2,1,0:T(2,128)} %bitcast.22, f32[1,128]{1,0:T(1,128)} %gain_ref.1, f32[8,128]{1,0:T(8,128)} %convert_bitcast_fusion.rt_ref, ...), custom_call_target="tpu_custom_call" | custom-call | tf_op jit(solution)/shard_map/moe_ring/pallas_call | solution.py:409
  197.9 1.2 slice_bitcast_fusion
  199.1 1.5 copy.12

commit v2 on v1

v2 whole, which is shorter than its diff:
```python
import functools

import jax
import jax.numpy as jnp
from jax import lax
from jax.experimental import pallas as pl
from jax.experimental.pallas import tpu as pltpu
from jax.sharding import PartitionSpec as P

MESH = pl.DeviceIdType.MESH
GROUPS = 8
TOPK = 2
DRO_RATE = 0.3
LANES = 128
F32 = jnp.float32
BF16 = jnp.bfloat16
LAST_DIMS = (((1,), (1,)), ((), ()))


def dot(a, b):
    return jnp.dot(a, b, preferred_element_type=F32)


def dot_t(a, b):
    return lax.dot_general(a, b, LAST_DIMS, preferred_element_type=F32)


def ones_where(mask):
    return jnp.where(mask, 1.0, 0.0).astype(BF16)


def kernel(
    sections, experts, slots, sent, per_group, width,
    tok_ref, tgt_ref, gid_ref, ids_ref, gain_ref, rt_ref, wg_ref, wu_ref, wd_ref,
    grad_ref, loss_ref,
    w_gu, w_dn, x_all, x_res, out_buf, x_in, acc, sq_acc, logit_acc, act, dn_acc, part_out, part_in,
    tgt, gid, ids, ids_before, gain_row, rt_raw,
    pick, scat, member, upper, eye, rt_mine, rt_in, rt_bf, red_mine, red_in, red_z,
    in_sem, w_sem, wd_sem, wd_send, wd_recv, d_send, d_recv, f_send, f_recv, a_send, a_recv,
    c_send, c_recv, z_send, z_recv, r_send, r_recv, rf_send, rf_recv, i_send, i_recv, s_send, s_recv,
    sz_send, sz_recv,
):
    chips = experts * 2
    across = 4
    down = chips // across
    rows = tok_ref.shape[0]
    hidden = wg_ref.shape[-1]
    section = lax.axis_index("section")
    expert = lax.axis_index("expert")
    lane = lax.axis_index("dp")
    core = lax.rem(lane, 2)
    half = lane // 2
    x_place = lax.rem(expert, across)
    y_place = expert // across * 2 + half
    mine = expert * 2 + half
    other = 1 - core
    sibling = (section, expert, half * 2 + other)

    def hops(offset):
        return min(offset[0], across - offset[0]) + min(offset[1], down - offset[1])

    offsets = [(dx, dy) for dx in range(across) for dy in range(down)]
    order = [(0, 0)] + sorted(offsets[1:], key=lambda offset: -hops(offset))
    sends = order[1:] + order[:1]

    def chip(offset, sign=1):
        x = lax.rem(x_place + across + sign * offset[0], across)
        y = lax.rem(y_place + down + sign * offset[1], down)
        return y // 2 * across + x, lax.rem(y, 2)

    def place_of(offset, sign=1):
        e, h = chip(offset, sign)
        return e * 2 + h

    def device(offset, on=0, swap=0):
        e, h = chip(offset)
        return (lax.rem(section + on, sections), e, h * 2 + (other if swap else core))

    def remote(src, dst, send, recv, target):
        return pltpu.make_async_remote_copy(
            src_ref=src, dst_ref=dst, send_sem=send, recv_sem=recv, device_id=target, device_id_type=MESH
        )

    inputs = [
        pltpu.make_async_copy(src, dst, in_sem.at[n])
        for n, (src, dst) in enumerate(
            [(ids_ref, ids), (tok_ref, x_all.at[0]), (gain_ref, gain_row), (rt_ref, rt_raw), (tgt_ref, tgt), (gid_ref, gid)]
        )
    ]
    loads = []
    for side in range(2):
        loads.append(pltpu.make_async_copy(wg_ref.at[:, side], w_gu.at[side, :, :, 0:hidden], w_sem.at[2 * side]))
        loads.append(
            pltpu.make_async_copy(wu_ref.at[:, side], w_gu.at[side, :, :, hidden : 2 * hidden], w_sem.at[2 * side + 1])
        )
    for j in range(chips):
        own_columns = pl.ds(pl.multiple_of(j * 2 * LANES + core * LANES, LANES), LANES)
        loads.append(pltpu.make_async_copy(wd_ref.at[:, own_columns], w_dn.at[core, j], wd_sem.at[j]))
    for load in inputs + loads:
        load.start()

    part_in[...] = jnp.zeros(part_in.shape, BF16)

    barrier = pltpu.get_barrier_semaphore()
    partners = {(dx, dy, 0, 0) for dx, dy in offsets[1:]} | {(0, 0, 0, 1)}
    partners |= {(dx, dy, dz % sections, 0) for dx, dy in offsets for dz in (1, -1)}
    partners |= {(0, 0, dz, swap) for dz in range(1, sections) for swap in range(2)}
    for dx, dy, dz, swap in sorted(partners):
        pl.semaphore_signal(barrier, inc=1, device_id=device((dx, dy), dz, swap), device_id_type=MESH)

    first = lax.broadcasted_iota(jnp.int32, (rows, rows), 0)
    second = lax.broadcasted_iota(jnp.int32, (rows, rows), 1)
    upper[...] = ones_where(first < second)
    eye[...] = ones_where(first == second)
    for load in inputs:
        load.wait()
    gain = gain_row[...]
    rt_mine[0:8, :] = rt_raw[...].astype(F32)
    rt_mine[8:16, :] = jnp.broadcast_to(1.0 / (gain * gain), (8, LANES))
    rt_in[core, 0] = rt_mine[...]

    expert_rows = lax.broadcasted_iota(jnp.int32, (16, rows), 0)

    def micro_of(moment):
        return lax.rem(section + 2 * sections - moment, sections)

    def ranks(table, micro):
        first_id = table[micro, 0:1, :]
        second_id = table[micro, 1:2, :]
        hit_first = first_id == expert_rows
        hit_second = second_id == expert_rows
        either = hit_first | hit_second
        named = ones_where(either)
        return first_id, second_id, hit_first, hit_second, either, named, dot(named, upper[...])

    def prepare_pick(moment):
        _, _, _, _, either, named, rank = ranks(ids, micro_of(moment))
        member[...] = named
        key = jnp.where(either, rank, -1.0)
        slot_rows = lax.broadcasted_iota(jnp.int32, (slots, rows), 0).astype(F32)
        for e in range(experts):
            pick[e * slots : (e + 1) * slots, :] = ones_where(key[e : e + 1, :] == slot_rows)

    def prepare_scatter(moment):
        first_id, second_id, hit_first, hit_second, _, _, rank = ranks(ids_before, micro_of(moment))
        rank_first = jnp.sum(jnp.where(hit_first, rank, 0.0), axis=0, keepdims=True)
        rank_second = jnp.sum(jnp.where(hit_second, rank, 0.0), axis=0, keepdims=True)
        table = jnp.where(expert_rows == 0, first_id.astype(F32), second_id.astype(F32))
        table = jnp.where(expert_rows == 2, rank_first, table)
        table = jnp.where(expert_rows == 3, rank_second, table)
        spread = dot_t(eye[...], table.astype(BF16))
        slot_first = spread[:, 0:1] * slots + spread[:, 2:3]
        slot_second = spread[:, 1:2] * slots + spread[:, 3:4]
        lanes = lax.broadcasted_iota(jnp.int32, (rows, LANES), 1).astype(F32)
        for n in range(experts * slots // LANES):
            here = lanes + float(n * LANES)
            scat[:, n * LANES : (n + 1) * LANES] = ones_where((slot_first == here) | (slot_second == here))

    prepare_pick(0)

    pl.semaphore_wait(barrier, len(partners))

    def router_copy(k):
        return remote(rt_mine, rt_in.at[core, k], r_send.at[k], r_recv.at[k], device(order[k]))

    ids_copy = remote(ids, ids_before, i_send.at[0], i_recv.at[0], device((0, 0), 1))

    def down_copy(j):
        sib_columns = pl.ds(pl.multiple_of(j * 2 * LANES + other * LANES, LANES), LANES)
        return remote(wd_ref.at[:, sib_columns], w_dn.at[core, j], wd_send.at[j], wd_recv.at[j], sibling)

    for k in range(1, chips):
        router_copy(k).start()
    ids_copy.start()

    def dispatch_copy(k, side):
        e, _ = chip(order[k])
        block = pl.ds(pl.multiple_of(e * slots, 16), sent)
        return remote(
            out_buf.at[block, :], x_in.at[side, core, k, pl.ds(0, sent)], d_send.at[k], d_recv.at[side, k],
            device(order[k]),
        )

    def dispatch(moment, side):
        scaled = (x_all[moment].astype(F32) * gain).astype(BF16)
        out_buf[...] = dot(pick[...], scaled).astype(BF16)
        for k in range(1, chips):
            dispatch_copy(k, side).start()
        own_block = pl.ds(pl.multiple_of(expert * slots, 16), slots)
        x_in[side, core, 0] = out_buf[own_block, :]

    def first_tick():
        for j in range(chips):
            down_copy(j).start()
        for k in range(1, chips):
            copy = router_copy(k)
            copy.wait_recv()
            copy.wait_send()
        forward = remote(rt_in.at[core], rt_in.at[core], rf_send.at[0], rf_recv.at[0], sibling)
        forward.start()
        ids_copy.wait_recv()
        ids_copy.wait_send()
        forward.wait_send()
        remote(rt_in.at[other], rt_in.at[other], rf_send.at[0], rf_recv.at[0], sibling).wait_recv()
        for side in range(2):
            for k in range(chips):
                rt_bf[side, :, k * LANES : (k + 1) * LANES] = rt_in[side, k].astype(BF16)
        for load in loads:
            load.wait()

    def down_here():
        for j in range(chips):
            copy = remote(wd_ref.at[:, pl.ds(0, LANES)], w_dn.at[other, j], wd_send.at[j], wd_recv.at[j], sibling)
            copy.wait_send()
            copy.wait_recv()

    group_count = chips // per_group

    def group_work(side, source, g, fresh):
        ks = range(g * per_group, (g + 1) * per_group)
        blocks = [x_in[side, source, k] for k in ks]
        block = jnp.concatenate(blocks, axis=1)
        weight = jnp.concatenate([w_gu[source, place_of(order[k], -1)] for k in ks], axis=0)
        product = dot(block, weight)
        router = rt_bf[source, :, g * per_group * LANES : (g + 1) * per_group * LANES]
        logits = dot_t(block, router)
        squares = None
        for k, piece in zip(ks, blocks):
            wide = piece.astype(F32)
            term = wide * wide * rt_in[source, k, 8:9, :]
            squares = term if squares is None else squares + term
        if fresh:
            acc[...] = product
            logit_acc[...] = logits
            sq_acc[...] = squares
        else:
            acc[...] += product
            logit_acc[...] += logits
            sq_acc[...] += squares

    def forward_copy(source, g, side):
        block = x_in.at[side, source, pl.ds(g * per_group, per_group)]
        return remote(block, block, f_send.at[g], f_recv.at[side, g], sibling)

    def own_group(g, side, fresh=False):
        for k in range(max(1, g * per_group), (g + 1) * per_group):
            dispatch_copy(k, side).wait_recv()
        forward_copy(core, g, side).start()
        group_work(side, core, g, fresh)

    def sibling_group(g, side):
        forward_copy(other, g, side).wait_recv()
        group_work(side, other, g, False)

    pairs = [(n, n + 1) for n in range(0, chips, 2)]

    def tick(moment, carry):
        side = lax.rem(moment, 2)
        dispatch(moment, side)
        ahead = remote(
            x_all.at[moment], x_res.at[moment], z_send.at[0], z_recv.at[moment], device((0, 0), 1)
        )
        ahead.start()

        @pl.when(moment == 0)
        def _():
            first_tick()

        prepare_scatter(moment + 1)

        own_group(0, side, True)
        for g in range(1, group_count):
            own_group(g, side)
            sibling_group(g - 1, side)
        sibling_group(group_count - 1, side)

        row_scale = lax.rsqrt(jnp.sum(sq_acc[...], axis=1, keepdims=True) / width + 1e-6)
        gate_part = acc[:, 0:hidden] * row_scale
        up_part = acc[:, hidden : 2 * hidden] * row_scale
        act[core] = (gate_part / (1.0 + jnp.exp(-gate_part)) * up_part).astype(BF16)
        swap = remote(act.at[core], act.at[core], a_send.at[0], a_recv.at[0], sibling)
        swap.start()

        own_pick = pick[pl.ds(pl.multiple_of(expert * slots, 16), slots), :]
        chosen = dot_t(own_pick, member[...]) > 0.5
        logits = logit_acc[...] * row_scale
        lanes = lax.broadcasted_iota(jnp.int32, (slots, 16), 1)
        top = jnp.max(jnp.where(chosen, logits, -1e30), axis=1, keepdims=True)
        raised = jnp.where(chosen, jnp.exp(jnp.where(chosen, logits - top, 0.0)), 0.0)
        gate = jnp.sum(jnp.where(lanes == expert, raised, 0.0), axis=1, keepdims=True) / jnp.maximum(
            jnp.sum(raised, axis=1, keepdims=True), 1e-30
        )

        def down_weight(source, pair):
            return jnp.concatenate([w_dn[source, place_of(sends[n])] for n in pair], axis=1)

        own_act = act[core]
        for i, pair in enumerate(pairs):
            dn_acc[i] = dot(own_act, down_weight(core, pair))
        for g in range(group_count):
            forward_copy(core, g, side).wait_send()
        for k in range(1, chips):
            dispatch_copy(k, side).wait_send()

        @pl.when(moment == 0)
        def _():
            down_here()

        remote(act.at[other], act.at[other], a_send.at[0], a_recv.at[0], sibling).wait_recv()
        swap.wait_send()
        sib_act = act[other]
        landing = half * experts + expert

        def part_copy(n):
            return remote(
                part_out.at[n, pl.ds(0, sent)], part_in.at[moment, landing, pl.ds(0, sent)], c_send.at[n],
                c_recv.at[moment], device(sends[n], 1),
            )

        for i, pair in enumerate(pairs):
            piece = ((dn_acc[i] + dot(sib_act, down_weight(other, pair))) * gate).astype(BF16)
            for at, n in enumerate(pair):
                part_out[n] = piece[:, at * LANES : (at + 1) * LANES]
                part_copy(n).start()

        prepare_pick(moment + 1)

        for n in range(chips):
            part_copy(n).wait_send()
        ahead.wait_send()
        ahead.wait_recv()
        everything = part_in.at[moment, :, pl.ds(0, sent)]
        remote(everything, everything, c_send.at[0], c_recv.at[moment], device((0, 0), 1)).wait_recv()
        table = scat[...]
        count = experts * slots
        parts = part_in[moment].reshape(chips * slots, LANES)
        moe = dot(table, parts[0:count]) + dot(table, parts[count : 2 * count])
        x_all[moment + 1] = (x_res[moment].astype(F32) + moe).astype(BF16)
        return carry

    lax.fori_loop(0, sections, tick, 0)

    difference = x_all[sections].astype(F32) - tgt[...].astype(F32)
    row_loss = jnp.sum(difference * difference, axis=1, keepdims=True) / width
    group_column = dot_t(eye[...], jnp.broadcast_to(gid[...].astype(F32), (16, rows)).astype(BF16))[:, 0:1]
    lanes = lax.broadcasted_iota(jnp.int32, (rows, LANES), 1).astype(F32)
    belongs = jnp.where(group_column == lanes, 1.0, 0.0)
    totals = jnp.sum(belongs * row_loss, axis=0, keepdims=True)
    counts = jnp.sum(belongs, axis=0, keepdims=True)
    red_rows = lax.broadcasted_iota(jnp.int32, (8, LANES), 0)
    local = jnp.where(red_rows == 0, totals, counts)
    red_mine[0] = local
    red_in[mine] = local

    def plane_copy(k, place):
        return remote(red_mine.at[0], red_in.at[place], s_send.at[k], s_recv.at[k], device(order[k]))

    for k in range(1, chips):
        plane_copy(k, mine).start()
    for k in range(1, chips):
        copy = plane_copy(k, place_of(order[k], -1))
        copy.wait_recv()
        copy.wait_send()
    plane = red_in[0]
    for j in range(1, chips):
        plane = plane + red_in[j]
    red_mine[1] = plane
    red_z[core, section] = plane
    steps = [(dz, swap) for dz in range(sections) for swap in range(2) if dz or swap]

    def depth_copy(n, lane_core, place):
        dz, swap = steps[n]
        return remote(
            red_mine.at[1], red_z.at[lane_core, place], sz_send.at[n], sz_recv.at[n], device((0, 0), dz, swap)
        )

    for n in range(len(steps)):
        depth_copy(n, core, section).start()
    for n, (dz, swap) in enumerate(steps):
        copy = depth_copy(n, other if swap else core, lax.rem(section + sections - dz, sections))
        copy.wait_recv()
        copy.wait_send()
    whole = red_z[0, 0]
    for n in range(1, 2 * sections):
        whole = whole + red_z[n // sections, n % sections]
    total = whole[0:1, :]
    count = whole[1:2, :] / (chips * 2)
    safe = jnp.maximum(count, 1.0)
    group_loss = total / safe
    lane_row = lax.broadcasted_iota(jnp.int32, (1, LANES), 1)
    raised = jnp.where(lane_row < GROUPS, jnp.exp(DRO_RATE * group_loss), 0.0)
    weight = raised / jnp.sum(raised, axis=1, keepdims=True) * (sections * rows) / safe
    row_weight = jnp.sum(belongs * weight, axis=1, keepdims=True)
    grad_ref[...] = (row_weight * difference).astype(BF16)
    loss_ref[...] = group_loss[:, 0:GROUPS]


def per_device(
    slots, sent, per_group, tokens, targets, group_ids, expert_ids, norm_gain, router, w_gate, w_up, w_down
):
    sections = lax.axis_size("section")
    experts = lax.axis_size("expert")
    chips = experts * 2
    groups = chips // per_group
    rows = tokens.shape[1]
    width = w_gate.shape[2]
    hidden = w_gate.shape[3]
    choices = jnp.transpose(expert_ids[0, 0], (0, 2, 1))
    router_rows = jnp.transpose(router[0])
    if experts < 8:
        router_rows = jnp.zeros((8, LANES), BF16).at[:experts].set(router_rows)
    vmem = pl.BlockSpec(memory_space=pltpu.VMEM)
    anywhere = pl.BlockSpec(memory_space=pl.ANY)
    dma = pltpu.SemaphoreType.DMA
    scratch = [
        pltpu.VMEM((2, chips, LANES, 2 * hidden), BF16),
        pltpu.VMEM((2, chips, hidden, LANES), BF16),
        pltpu.VMEM((sections + 1, rows, LANES), BF16),
        pltpu.VMEM((sections, rows, LANES), BF16),
        pltpu.VMEM((experts * slots, LANES), BF16),
        pltpu.VMEM((2, 2, chips, slots, LANES), BF16),
        pltpu.VMEM((slots, 2 * hidden), F32),
        pltpu.VMEM((slots, LANES), F32),
        pltpu.VMEM((slots, 16), F32),
        pltpu.VMEM((2, slots, hidden), BF16),
        pltpu.VMEM((chips // 2, slots, 2 * LANES), F32),
        pltpu.VMEM((chips, slots, LANES), BF16),
        pltpu.VMEM((sections, chips, slots, LANES), BF16),
        pltpu.VMEM((rows, LANES), BF16),
        pltpu.VMEM((1, rows), jnp.int32),
        pltpu.VMEM((sections, 2, rows), jnp.int32),
        pltpu.VMEM((sections, 2, rows), jnp.int32),
        pltpu.VMEM((1, LANES), F32),
        pltpu.VMEM((8, LANES), BF16),
        pltpu.VMEM((experts * slots, rows), BF16),
        pltpu.VMEM((rows, experts * slots), BF16),
        pltpu.VMEM((16, rows), BF16),
        pltpu.VMEM((rows, rows), BF16),
        pltpu.VMEM((rows, rows), BF16),
        pltpu.VMEM((16, LANES), F32),
        pltpu.VMEM((2, chips, 16, LANES), F32),
        pltpu.VMEM((2, 16, chips * LANES), BF16),
        pltpu.VMEM((2, 8, LANES), F32),
        pltpu.VMEM((chips, 8, LANES), F32),
        pltpu.VMEM((2, sections, 8, LANES), F32),
        dma((6,)),
        dma((4,)),
        dma((chips,)),
        dma((chips,)),
        dma((chips,)),
        dma((chips,)),
        dma((2, chips)),
        dma((groups,)),
        dma((2, groups)),
        dma((1,)),
        dma((1,)),
        dma((chips,)),
        dma((sections,)),
        dma((1,)),
        dma((sections,)),
        dma((chips,)),
        dma((chips,)),
        dma((1,)),
        dma((1,)),
        dma((1,)),
        dma((1,)),
        dma((chips,)),
        dma((chips,)),
        dma((2 * sections - 1,)),
        dma((2 * sections - 1,)),
    ]
    grad, loss = pl.pallas_call(
        functools.partial(kernel, sections, experts, slots, sent, per_group, float(width)),
        out_shape=(
            jax.ShapeDtypeStruct((rows, LANES), BF16),
            jax.ShapeDtypeStruct((1, GROUPS), F32),
        ),
        in_specs=[anywhere] * 9,
        out_specs=(vmem, vmem),
        scratch_shapes=scratch,
        compiler_params=pltpu.CompilerParams(
            collective_id=0, has_side_effects=True, vmem_limit_bytes=60 * 1024 * 1024
        ),
        name="moe_ring",
    )(
        tokens[0],
        targets[0],
        group_ids,
        choices,
        norm_gain,
        router_rows,
        w_gate.reshape(chips, 2, LANES, hidden),
        w_up.reshape(chips, 2, LANES, hidden),
        w_down.reshape(hidden, width),
    )
    return grad[None], loss[0]


def build(mesh, slots, sent, per_group):
    placed = (
        P("section", None, ("expert", "dp")),
        P("section", None, ("expert", "dp")),
        P("section", None),
        P(None, "section", None, None, None),
        P("section", ("expert", "dp")),
        P("section", ("expert", "dp"), None),
        P("section", "expert", None, "dp"),
        P("section", "expert", None, "dp"),
        P("section", "expert", "dp", None),
    )
    return jax.shard_map(
        functools.partial(per_device, slots, sent, per_group),
        mesh=mesh,
        in_specs=placed,
        out_specs=(P("section", None, ("expert", "dp")), P()),
        check_vma=False,
    )


def solution(mesh):
    return build(mesh, 80, 72, 4)
```

time: 201 us -> 187 us (0.930)
  Pallas kernels: 196 us -> 184 us
    pallas_call x1, Pallas kernels: 196 us -> 184 us  [per_device(): pl.pallas_call(functools.partial(kernel, sections, experts, slots, sent,...]
where the time goes in v2:
time: 187 us
  Pallas kernels  184 us (98%)
  local copies, waits for them, and re-layouts  2.59 us (1%)
    pallas_call x1, Pallas kernels, per_device(): pl.pallas_call(functools.partial(kernel, sections, experts, slots, sent,...  184 us

profile of v2, /device:TPU:1, one launch (start us, length us, event | category | flops | bytes accessed | tf_op | source)
XLA Modules:
  0.0 187.3 jit_solution(8776606898473174655)
XLA Ops:
  0.6 184.0 %moe_ring.1 = (bf16[256,128]{1,0:T(8,128)(2,1)}, f32[1,8]{1,0:T(1,128)}) custom-call(bf16[256,128]{1,0:T(8,128)(2,1)} %bitcast.16, bf16[256,128]{1,0:T(8,128)(2,1)} %bitcast.17, s32[1,256]{1,0:T(1,128)} %gid_ref.1, s32[8,2,256]{2,1,0:T(2,128)} %bitcast.19, f32[1,128]{1,0:T(1,128)} %gain_ref.1, bf16[8,128]{1,0:T(8,128)(2,1)} %bitcast.20, ...), custom_call_target="tpu_custom_call" | custom-call | tf_op jit(solution)/shard_map/moe_ring/pallas_call | solution.py:472
  184.7 1.5 copy.13
  186.1 1.1 copy.14

commit v3 on v2

--- a/solution.py
+++ b/solution.py
@@ -34,11 +34,11 @@
     tok_ref, tgt_ref, gid_ref, ids_ref, gain_ref, rt_ref, wg_ref, wu_ref, wd_ref,
     grad_ref, loss_ref,
     w_gu, w_dn, x_all, x_res, out_buf, x_in, acc, sq_acc, logit_acc, act, dn_acc, part_out, part_in,
-    tgt, gid, ids, ids_before, gain_row, rt_raw,
-    pick, scat, member, upper, eye, rt_mine, rt_in, rt_bf, red_mine, red_in, red_z,
+    tgt, gid, ids, gain_row, rt_raw, tgt_near, gid_near, ids_near, gain_near, ids_out, ids_back, gain_out, x_last,
+    pick, scat, chosen_mask, upper, eye, rt_mine, rt_in, rt_bf, red_mine, red_in, red_z,
     in_sem, w_sem, wd_sem, wd_send, wd_recv, d_send, d_recv, f_send, f_recv, a_send, a_recv,
-    c_send, c_recv, z_send, z_recv, r_send, r_recv, rf_send, rf_recv, i_send, i_recv, s_send, s_recv,
-    sz_send, sz_recv,
+    c_send, c_recv, c_own, z_send, z_recv, r_send, r_recv, rf_send, rf_recv, n_send, n_recv, s_send, s_recv,
+    sz_send, sz_recv, l_send, l_recv,
 ):
     chips = experts * 2
     across = 4
@@ -118,11 +118,14 @@
     rt_mine[0:8, :] = rt_raw[...].astype(F32)
     rt_mine[8:16, :] = jnp.broadcast_to(1.0 / (gain * gain), (8, LANES))
     rt_in[core, 0] = rt_mine[...]
+    gain_out[...] = gain
 
     expert_rows = lax.broadcasted_iota(jnp.int32, (16, rows), 0)
 
-    def micro_of(moment):
-        return lax.rem(section + 2 * sections - moment, sections)
+    slot_rows = lax.broadcasted_iota(jnp.int32, (slots, rows), 0).astype(F32)
+
+    def micro_of(place):
+        return lax.rem(place + 2 * sections, sections)
 
     def ranks(table, micro):
         first_id = table[micro, 0:1, :]
@@ -133,16 +136,21 @@
         named = ones_where(either)
         return first_id, second_id, hit_first, hit_second, either, named, dot(named, upper[...])
 
-    def prepare_pick(moment):
-        _, _, _, _, either, named, rank = ranks(ids, micro_of(moment))
-        member[...] = named
+    def prepare_pick(table, micro):
+        _, _, _, _, either, _, rank = ranks(table, micro)
         key = jnp.where(either, rank, -1.0)
-        slot_rows = lax.broadcasted_iota(jnp.int32, (slots, rows), 0).astype(F32)
         for e in range(experts):
             pick[e * slots : (e + 1) * slots, :] = ones_where(key[e : e + 1, :] == slot_rows)
 
+    def prepare_mask(moment):
+        _, _, _, _, either, named, rank = ranks(ids, micro_of(section - moment))
+        key = jnp.sum(jnp.where(expert_rows == expert, jnp.where(either, rank, -1.0), 0.0), axis=0, keepdims=True)
+        chosen_mask[...] = dot_t(ones_where(key == slot_rows), named)
+
     def prepare_scatter(moment):
-        first_id, second_id, hit_first, hit_second, _, _, rank = ranks(ids_before, micro_of(moment))
+        first_id, second_id, hit_first, hit_second, _, _, rank = ranks(
+            ids_back, micro_of(section + core - 1 - moment)
+        )
         rank_first = jnp.sum(jnp.where(hit_first, rank, 0.0), axis=0, keepdims=True)
         rank_second = jnp.sum(jnp.where(hit_second, rank, 0.0), axis=0, keepdims=True)
         table = jnp.where(expert_rows == 0, first_id.astype(F32), second_id.astype(F32))
@@ -156,14 +164,18 @@
             here = lanes + float(n * LANES)
             scat[:, n * LANES : (n + 1) * LANES] = ones_where((slot_first == here) | (slot_second == here))
 
-    prepare_pick(0)
+    prepare_pick(ids, section)
 
     pl.semaphore_wait(barrier, len(partners))
 
     def router_copy(k):
         return remote(rt_mine, rt_in.at[core, k], r_send.at[k], r_recv.at[k], device(order[k]))
 
-    ids_copy = remote(ids, ids_before, i_send.at[0], i_recv.at[0], device((0, 0), 1))
+    toward = device((0, 0), sections + 1 - 2 * core)
+    neighbour = [
+        remote(src, dst, n_send.at[n], n_recv.at[n], toward)
+        for n, (src, dst) in enumerate([(ids, ids_near), (gain_row, gain_near), (gid, gid_near), (tgt, tgt_near)])
+    ]
 
     def down_copy(j):
         sib_columns = pl.ds(pl.multiple_of(j * 2 * LANES + other * LANES, LANES), LANES)
@@ -171,23 +183,36 @@
 
     for k in range(1, chips):
         router_copy(k).start()
-    ids_copy.start()
-
-    def dispatch_copy(k, side):
+    for copy in neighbour:
+        copy.start()
+
+    def begun(moment):
+        return 1 - (sections - moment) // sections
+
+    def stays(moment):
+        return core * begun(moment) == 0
+
+    def dispatch_copy(k, moment):
         e, _ = chip(order[k])
         block = pl.ds(pl.multiple_of(e * slots, 16), sent)
         return remote(
-            out_buf.at[block, :], x_in.at[side, core, k, pl.ds(0, sent)], d_send.at[k], d_recv.at[side, k],
-            device(order[k]),
-        )
-
-    def dispatch(moment, side):
-        scaled = (x_all[moment].astype(F32) * gain).astype(BF16)
+            out_buf.at[block, :], x_in.at[moment, core, k, pl.ds(0, sent)], d_send.at[k], d_recv.at[moment, k],
+            device(order[k], core * begun(moment)),
+        )
+
+    def dispatch(moment):
+        scaled = (x_all[moment].astype(F32) * gain_out[...]).astype(BF16)
         out_buf[...] = dot(pick[...], scaled).astype(BF16)
         for k in range(1, chips):
-            dispatch_copy(k, side).start()
-        own_block = pl.ds(pl.multiple_of(expert * slots, 16), slots)
-        x_in[side, core, 0] = out_buf[own_block, :]
+            dispatch_copy(k, moment).start()
+
+        @pl.when(stays(moment))
+        def _():
+            x_in[moment, core, 0] = out_buf[pl.ds(pl.multiple_of(expert * slots, 16), slots), :]
+
+        @pl.when(jnp.logical_not(stays(moment)))
+        def _():
+            dispatch_copy(0, moment).start()
 
     def first_tick():
         for j in range(chips):
@@ -198,8 +223,12 @@
             copy.wait_send()
         forward = remote(rt_in.at[core], rt_in.at[core], rf_send.at[0], rf_recv.at[0], sibling)
         forward.start()
-        ids_copy.wait_recv()
-        ids_copy.wait_send()
+        for copy in neighbour:
+            copy.wait_recv()
+            copy.wait_send()
+        ids_out[...] = jnp.where(core == 0, ids[...], ids_near[...])
+        ids_back[...] = jnp.where(core == 0, ids_near[...], ids[...])
+        gain_out[...] = jnp.where(core == 0, gain_row[...], gain_near[...])
         forward.wait_send()
         remote(rt_in.at[other], rt_in.at[other], rf_send.at[0], rf_recv.at[0], sibling).wait_recv()
         for side in range(2):
@@ -216,9 +245,9 @@
 
     group_count = chips // per_group
 
-    def group_work(side, source, g, fresh):
+    def group_work(moment, source, g, fresh):
         ks = range(g * per_group, (g + 1) * per_group)
-        blocks = [x_in[side, source, k] for k in ks]
+        blocks = [x_in[moment, source, k] for k in ks]
         block = jnp.concatenate(blocks, axis=1)
         weight = jnp.concatenate([w_gu[source, place_of(order[k], -1)] for k in ks], axis=0)
         product = dot(block, weight)
@@ -238,25 +267,30 @@
             logit_acc[...] += logits
             sq_acc[...] += squares
 
-    def forward_copy(source, g, side):
-        block = x_in.at[side, source, pl.ds(g * per_group, per_group)]
-        return remote(block, block, f_send.at[g], f_recv.at[side, g], sibling)
-
-    def own_group(g, side, fresh=False):
+    def forward_copy(source, g, moment):
+        block = x_in.at[moment, source, pl.ds(g * per_group, per_group)]
+        return remote(block, block, f_send.at[g], f_recv.at[g], sibling)
+
+    def own_group(g, moment, fresh=False):
+        if g == 0:
+
+            @pl.when(jnp.logical_not(stays(moment)))
+            def _():
+                dispatch_copy(0, moment).wait_recv()
+
         for k in range(max(1, g * per_group), (g + 1) * per_group):
-            dispatch_copy(k, side).wait_recv()
-        forward_copy(core, g, side).start()
-        group_work(side, core, g, fresh)
-
-    def sibling_group(g, side):
-        forward_copy(other, g, side).wait_recv()
-        group_work(side, other, g, False)
+            dispatch_copy(k, moment).wait_recv()
+        forward_copy(core, g, moment).start()
+        group_work(moment, core, g, fresh)
+
+    def sibling_group(g, moment):
+        forward_copy(other, g, moment).wait_recv()
+        group_work(moment, other, g, False)
 
     pairs = [(n, n + 1) for n in range(0, chips, 2)]
 
     def tick(moment, carry):
-        side = lax.rem(moment, 2)
-        dispatch(moment, side)
+        dispatch(moment)
         ahead = remote(
             x_all.at[moment], x_res.at[moment], z_send.at[0], z_recv.at[moment], device((0, 0), 1)
         )
@@ -266,13 +300,14 @@
         def _():
             first_tick()
 
-        prepare_scatter(moment + 1)
-
-        own_group(0, side, True)
+        prepare_mask(moment)
+        prepare_scatter(moment)
+
+        own_group(0, moment, True)
         for g in range(1, group_count):
-            own_group(g, side)
-            sibling_group(g - 1, side)
-        sibling_group(group_count - 1, side)
+            own_group(g, moment)
+            sibling_group(g - 1, moment)
+        sibling_group(group_count - 1, moment)
 
         row_scale = lax.rsqrt(jnp.sum(sq_acc[...], axis=1, keepdims=True) / width + 1e-6)
         gate_part = acc[:, 0:hidden] * row_scale
@@ -281,8 +316,7 @@
         swap = remote(act.at[core], act.at[core], a_send.at[0], a_recv.at[0], sibling)
         swap.start()
 
-        own_pick = pick[pl.ds(pl.multiple_of(expert * slots, 16), slots), :]
-        chosen = dot_t(own_pick, member[...]) > 0.5
+        chosen = chosen_mask[...] > 0.5
         logits = logit_acc[...] * row_scale
         lanes = lax.broadcasted_iota(jnp.int32, (slots, 16), 1)
         top = jnp.max(jnp.where(chosen, logits, -1e30), axis=1, keepdims=True)
@@ -298,9 +332,13 @@
         for i, pair in enumerate(pairs):
             dn_acc[i] = dot(own_act, down_weight(core, pair))
         for g in range(group_count):
-            forward_copy(core, g, side).wait_send()
+            forward_copy(core, g, moment).wait_send()
         for k in range(1, chips):
-            dispatch_copy(k, side).wait_send()
+            dispatch_copy(k, moment).wait_send()
+
+        @pl.when(jnp.logical_not(stays(moment)))
+        def _():
+            dispatch_copy(0, moment).wait_send()
 
         @pl.when(moment == 0)
         def _():
@@ -314,37 +352,62 @@
         def part_copy(n):
             return remote(
                 part_out.at[n, pl.ds(0, sent)], part_in.at[moment, landing, pl.ds(0, sent)], c_send.at[n],
-                c_recv.at[moment], device(sends[n], 1),
+                c_own.at[moment] if n == chips - 1 else c_recv.at[moment], device(sends[n], 1 - core),
             )
 
         for i, pair in enumerate(pairs):
             piece = ((dn_acc[i] + dot(sib_act, down_weight(other, pair))) * gate).astype(BF16)
             for at, n in enumerate(pair):
-                part_out[n] = piece[:, at * LANES : (at + 1) * LANES]
-                part_copy(n).start()
-
-        prepare_pick(moment + 1)
-
-        for n in range(chips):
+                value = piece[:, at * LANES : (at + 1) * LANES]
+                part_out[n] = value
+                if n < chips - 1:
+                    part_copy(n).start()
+                else:
+
+                    @pl.when(core == 0)
+                    def _(n=n):
+                        part_copy(n).start()
+
+                    @pl.when(core == 1)
+                    def _(value=value):
+                        part_in[moment, landing, 0:sent, :] = value[0:sent, :]
+
+        prepare_pick(ids_out, micro_of(section + core - moment - 1))
+
+        for n in range(chips - 1):
             part_copy(n).wait_send()
+
+        @pl.when(core == 0)
+        def _():
+            part_copy(chips - 1).wait_send()
+            part_copy(chips - 1).wait_recv()
+
         ahead.wait_send()
         ahead.wait_recv()
-        everything = part_in.at[moment, :, pl.ds(0, sent)]
+        everything = part_in.at[moment, pl.ds(0, chips - 1), pl.ds(0, sent)]
         remote(everything, everything, c_send.at[0], c_recv.at[moment], device((0, 0), 1)).wait_recv()
         table = scat[...]
         count = experts * slots
         parts = part_in[moment].reshape(chips * slots, LANES)
         moe = dot(table, parts[0:count]) + dot(table, parts[count : 2 * count])
-        x_all[moment + 1] = (x_res[moment].astype(F32) + moe).astype(BF16)
+        kept = jnp.where(core * (1 - begun(moment)) == 1, x_all[0].astype(F32), x_res[moment].astype(F32))
+        x_all[moment + 1] = (kept + moe).astype(BF16)
         return carry
 
     lax.fori_loop(0, sections, tick, 0)
 
-    difference = x_all[sections].astype(F32) - tgt[...].astype(F32)
-    row_loss = jnp.sum(difference * difference, axis=1, keepdims=True) / width
-    group_column = dot_t(eye[...], jnp.broadcast_to(gid[...].astype(F32), (16, rows)).astype(BF16))[:, 0:1]
+    last = remote(x_all.at[sections], x_last, l_send.at[0], l_recv.at[0], device((0, 0), 1))
+    last.start()
     lanes = lax.broadcasted_iota(jnp.int32, (rows, LANES), 1).astype(F32)
-    belongs = jnp.where(group_column == lanes, 1.0, 0.0)
+
+    def members(group_row):
+        column = dot_t(eye[...], jnp.broadcast_to(group_row.astype(F32), (16, rows)).astype(BF16))[:, 0:1]
+        return jnp.where(column == lanes, 1.0, 0.0)
+
+    aim = jnp.where(core == 0, tgt[...].astype(F32), tgt_near[...].astype(F32))
+    error = x_all[sections].astype(F32) - aim
+    row_loss = jnp.sum(error * error, axis=1, keepdims=True) / width
+    belongs = members(jnp.where(core == 0, gid[...], gid_near[...]))
     totals = jnp.sum(belongs * row_loss, axis=0, keepdims=True)
     counts = jnp.sum(belongs, axis=0, keepdims=True)
     red_rows = lax.broadcasted_iota(jnp.int32, (8, LANES), 0)
@@ -390,7 +453,11 @@
     lane_row = lax.broadcasted_iota(jnp.int32, (1, LANES), 1)
     raised = jnp.where(lane_row < GROUPS, jnp.exp(DRO_RATE * group_loss), 0.0)
     weight = raised / jnp.sum(raised, axis=1, keepdims=True) * (sections * rows) / safe
-    row_weight = jnp.sum(belongs * weight, axis=1, keepdims=True)
+    row_weight = jnp.sum(members(gid[...]) * weight, axis=1, keepdims=True)
+    last.wait_send()
+    last.wait_recv()
+    final = jnp.where(core == 0, x_all[sections].astype(F32), x_last[...].astype(F32))
+    difference = final - tgt[...].astype(F32)
     grad_ref[...] = (row_weight * difference).astype(BF16)
     loss_ref[...] = group_loss[:, 0:GROUPS]
 
@@ -418,7 +485,7 @@
         pltpu.VMEM((sections + 1, rows, LANES), BF16),
         pltpu.VMEM((sections, rows, LANES), BF16),
         pltpu.VMEM((experts * slots, LANES), BF16),
-        pltpu.VMEM((2, 2, chips, slots, LANES), BF16),
+        pltpu.VMEM((sections, 2, chips, slots, LANES), BF16),
         pltpu.VMEM((slots, 2 * hidden), F32),
         pltpu.VMEM((slots, LANES), F32),
         pltpu.VMEM((slots, 16), F32),
@@ -429,12 +496,19 @@
         pltpu.VMEM((rows, LANES), BF16),
         pltpu.VMEM((1, rows), jnp.int32),
         pltpu.VMEM((sections, 2, rows), jnp.int32),
+        pltpu.VMEM((1, LANES), F32),
+        pltpu.VMEM((8, LANES), BF16),
+        pltpu.VMEM((rows, LANES), BF16),
+        pltpu.VMEM((1, rows), jnp.int32),
         pltpu.VMEM((sections, 2, rows), jnp.int32),
         pltpu.VMEM((1, LANES), F32),
-        pltpu.VMEM((8, LANES), BF16),
+        pltpu.VMEM((sections, 2, rows), jnp.int32),
+        pltpu.VMEM((sections, 2, rows), jnp.int32),
+        pltpu.VMEM((1, LANES), F32),
+        pltpu.VMEM((rows, LANES), BF16),
         pltpu.VMEM((experts * slots, rows), BF16),
         pltpu.VMEM((rows, experts * slots), BF16),
-        pltpu.VMEM((16, rows), BF16),
+        pltpu.VMEM((slots, 16), F32),
         pltpu.VMEM((rows, rows), BF16),
         pltpu.VMEM((rows, rows), BF16),
         pltpu.VMEM((16, LANES), F32),
@@ -449,25 +523,28 @@
         dma((chips,)),
         dma((chips,)),
         dma((chips,)),
-        dma((2, chips)),
+        dma((sections, chips)),
         dma((groups,)),
-        dma((2, groups)),
+        dma((groups,)),
         dma((1,)),
         dma((1,)),
         dma((chips,)),
         dma((sections,)),
-        dma((1,)),
         dma((sections,)),
-        dma((chips,)),
-        dma((chips,)),
-        dma((1,)),
-        dma((1,)),
-        dma((1,)),
-        dma((1,)),
+        dma((1,)),
+        dma((sections,)),
+        dma((chips,)),
+        dma((chips,)),
+        dma((1,)),
+        dma((1,)),
+        dma((4,)),
+        dma((4,)),
         dma((chips,)),
         dma((chips,)),
         dma((2 * sections - 1,)),
         dma((2 * sections - 1,)),
+        dma((1,)),
+        dma((1,)),
     ]
     grad, loss = pl.pallas_call(
         functools.partial(kernel, sections, experts, slots, sent, per_group, float(width)),

time: 187 us -> 172 us (0.920)
  Pallas kernels: 184 us -> 168 us
    pallas_call x1, Pallas kernels: 184 us -> 168 us  [per_device(): pl.pallas_call(functools.partial(kernel, sections, experts, slots, sent,...]
where the time goes in v3:
time: 172 us; the launch traced here: 171 us
  Pallas kernels  168 us (98%)
  local copies, waits for them, and re-layouts  2.59 us (2%)
    pallas_call x1, Pallas kernels, per_device(): pl.pallas_call(functools.partial(kernel, sections, experts, slots, sent,...  168 us

profile of v3, /device:TPU:1, one launch (start us, length us, event | category | flops | bytes accessed | tf_op | source)
XLA Modules:
  0.0 171.4 jit_solution(4237194284536085671)
XLA Ops:
  0.6 168.2 %moe_ring.1 = (bf16[256,128]{1,0:T(8,128)(2,1)}, f32[1,8]{1,0:T(1,128)}) custom-call(bf16[256,128]{1,0:T(8,128)(2,1)} %bitcast.16, bf16[256,128]{1,0:T(8,128)(2,1)} %bitcast.17, s32[1,256]{1,0:T(1,128)} %gid_ref.1, s32[8,2,256]{2,1,0:T(2,128)} %bitcast.19, f32[1,128]{1,0:T(1,128)} %gain_ref.1, bf16[8,128]{1,0:T(8,128)(2,1)} %bitcast.20, ...), custom_call_target="tpu_custom_call" | custom-call | tf_op jit(solution)/shard_map/moe_ring/pallas_call | solution.py:549
  168.8 1.5 copy.13
  170.3 1.1 copy.14

commit v4 on v3

--- a/solution.py
+++ b/solution.py
@@ -30,7 +30,7 @@
 
 
 def kernel(
-    sections, experts, slots, sent, per_group, width,
+    sections, experts, slots, sent, groups, spread_out, width,
     tok_ref, tgt_ref, gid_ref, ids_ref, gain_ref, rt_ref, wg_ref, wu_ref, wd_ref,
     grad_ref, loss_ref,
     w_gu, w_dn, x_all, x_res, out_buf, x_in, acc, sq_acc, logit_acc, act, dn_acc, part_out, part_in,
@@ -96,10 +96,10 @@
     for j in range(chips):
         own_columns = pl.ds(pl.multiple_of(j * 2 * LANES + core * LANES, LANES), LANES)
         loads.append(pltpu.make_async_copy(wd_ref.at[:, own_columns], w_dn.at[core, j], wd_sem.at[j]))
-    for load in inputs + loads:
+    for load in inputs:
         load.start()
 
-    part_in[...] = jnp.zeros(part_in.shape, BF16)
+    part_in[:, :, sent:slots, :] = jnp.zeros((sections, chips, slots - sent, LANES), BF16)
 
     barrier = pltpu.get_barrier_semaphore()
     partners = {(dx, dy, 0, 0) for dx, dy in offsets[1:]} | {(0, 0, 0, 1)}
@@ -107,6 +107,8 @@
     partners |= {(0, 0, dz, swap) for dz in range(1, sections) for swap in range(2)}
     for dx, dy, dz, swap in sorted(partners):
         pl.semaphore_signal(barrier, inc=1, device_id=device((dx, dy), dz, swap), device_id_type=MESH)
+    for load in loads:
+        load.start()
 
     first = lax.broadcasted_iota(jnp.int32, (rows, rows), 0)
     second = lax.broadcasted_iota(jnp.int32, (rows, rows), 1)
@@ -243,15 +245,16 @@
             copy.wait_send()
             copy.wait_recv()
 
-    group_count = chips // per_group
+    group_count = len(groups)
 
     def group_work(moment, source, g, fresh):
-        ks = range(g * per_group, (g + 1) * per_group)
+        start, stop = groups[g]
+        ks = range(start, stop)
         blocks = [x_in[moment, source, k] for k in ks]
         block = jnp.concatenate(blocks, axis=1)
         weight = jnp.concatenate([w_gu[source, place_of(order[k], -1)] for k in ks], axis=0)
         product = dot(block, weight)
-        router = rt_bf[source, :, g * per_group * LANES : (g + 1) * per_group * LANES]
+        router = rt_bf[source, :, start * LANES : stop * LANES]
         logits = dot_t(block, router)
         squares = None
         for k, piece in zip(ks, blocks):
@@ -268,7 +271,7 @@
             sq_acc[...] += squares
 
     def forward_copy(source, g, moment):
-        block = x_in.at[moment, source, pl.ds(g * per_group, per_group)]
+        block = x_in.at[moment, source, pl.ds(groups[g][0], groups[g][1] - groups[g][0])]
         return remote(block, block, f_send.at[g], f_recv.at[g], sibling)
 
     def own_group(g, moment, fresh=False):
@@ -278,7 +281,7 @@
             def _():
                 dispatch_copy(0, moment).wait_recv()
 
-        for k in range(max(1, g * per_group), (g + 1) * per_group):
+        for k in range(max(1, groups[g][0]), groups[g][1]):
             dispatch_copy(k, moment).wait_recv()
         forward_copy(core, g, moment).start()
         group_work(moment, core, g, fresh)
@@ -287,7 +290,7 @@
         forward_copy(other, g, moment).wait_recv()
         group_work(moment, other, g, False)
 
-    pairs = [(n, n + 1) for n in range(0, chips, 2)]
+    pairs = [tuple(range(n, n + spread_out)) for n in range(0, chips, spread_out)]
 
     def tick(moment, carry):
         dispatch(moment)
@@ -463,12 +466,11 @@
 
 
 def per_device(
-    slots, sent, per_group, tokens, targets, group_ids, expert_ids, norm_gain, router, w_gate, w_up, w_down
+    slots, sent, groups, spread_out, tokens, targets, group_ids, expert_ids, norm_gain, router, w_gate, w_up, w_down
 ):
     sections = lax.axis_size("section")
     experts = lax.axis_size("expert")
     chips = experts * 2
-    groups = chips // per_group
     rows = tokens.shape[1]
     width = w_gate.shape[2]
     hidden = w_gate.shape[3]
@@ -490,7 +492,7 @@
         pltpu.VMEM((slots, LANES), F32),
         pltpu.VMEM((slots, 16), F32),
         pltpu.VMEM((2, slots, hidden), BF16),
-        pltpu.VMEM((chips // 2, slots, 2 * LANES), F32),
+        pltpu.VMEM((chips // spread_out, slots, spread_out * LANES), F32),
         pltpu.VMEM((chips, slots, LANES), BF16),
         pltpu.VMEM((sections, chips, slots, LANES), BF16),
         pltpu.VMEM((rows, LANES), BF16),
@@ -524,8 +526,8 @@
         dma((chips,)),
         dma((chips,)),
         dma((sections, chips)),
-        dma((groups,)),
-        dma((groups,)),
+        dma((len(groups),)),
+        dma((len(groups),)),
         dma((1,)),
         dma((1,)),
         dma((chips,)),
@@ -547,7 +549,7 @@
         dma((1,)),
     ]
     grad, loss = pl.pallas_call(
-        functools.partial(kernel, sections, experts, slots, sent, per_group, float(width)),
+        functools.partial(kernel, sections, experts, slots, sent, groups, spread_out, float(width)),
         out_shape=(
             jax.ShapeDtypeStruct((rows, LANES), BF16),
             jax.ShapeDtypeStruct((1, GROUPS), F32),
@@ -573,7 +575,7 @@
     return grad[None], loss[0]
 
 
-def build(mesh, slots, sent, per_group):
+def build(mesh, slots, sent, groups, spread_out):
     placed = (
         P("section", None, ("expert", "dp")),
         P("section", None, ("expert", "dp")),
@@ -586,7 +588,7 @@
         P("section", "expert", "dp", None),
     )
     return jax.shard_map(
-        functools.partial(per_device, slots, sent, per_group),
+        functools.partial(per_device, slots, sent, groups, spread_out),
         mesh=mesh,
         in_specs=placed,
         out_specs=(P("section", None, ("expert", "dp")), P()),
@@ -595,4 +597,4 @@
 
 
 def solution(mesh):
-    return build(mesh, 80, 72, 4)
+    return build(mesh, 80, 72, ((0, 8), (8, 16)), 4)

time: 172 us -> 163 us (0.948)
  Pallas kernels: 168 us -> 159 us
    pallas_call x1, Pallas kernels: 168 us -> 159 us  [per_device(): pl.pallas_call(functools.partial(kernel, sections, experts, slots, sent,...]
where the time goes in v4:
time: 163 us; the launch traced here: 162 us
  Pallas kernels  159 us (98%)
  local copies, waits for them, and re-layouts  2.59 us (2%)
    pallas_call x1, Pallas kernels, per_device(): pl.pallas_call(functools.partial(kernel, sections, experts, slots, sent,...  159 us

profile of v4, /device:TPU:1, one launch (start us, length us, event | category | flops | bytes accessed | tf_op | source)
XLA Modules:
  0.0 162.3 jit_solution(5093238684193437521)
XLA Ops:
  0.6 159.1 %moe_ring.1 = (bf16[256,128]{1,0:T(8,128)(2,1)}, f32[1,8]{1,0:T(1,128)}) custom-call(bf16[256,128]{1,0:T(8,128)(2,1)} %bitcast.16, bf16[256,128]{1,0:T(8,128)(2,1)} %bitcast.17, s32[1,256]{1,0:T(1,128)} %gid_ref.1, s32[8,2,256]{2,1,0:T(2,128)} %bitcast.19, f32[1,128]{1,0:T(1,128)} %gain_ref.1, bf16[8,128]{1,0:T(8,128)(2,1)} %bitcast.20, ...), custom_call_target="tpu_custom_call" | custom-call | tf_op jit(solution)/shard_map/moe_ring/pallas_call | solution.py:551
  159.7 1.5 copy.13
  161.2 1.1 copy.14

commit v5 on v4

--- a/solution.py
+++ b/solution.py
@@ -216,6 +216,13 @@
         def _():
             dispatch_copy(0, moment).start()
 
+    def router_forward(source):
+        return remote(rt_in.at[source], rt_in.at[source], rf_send.at[0], rf_recv.at[0], sibling)
+
+    def round_router(source):
+        for k in range(chips):
+            rt_bf[source, :, k * LANES : (k + 1) * LANES] = rt_in[source, k].astype(BF16)
+
     def first_tick():
         for j in range(chips):
             down_copy(j).start()
@@ -223,21 +230,21 @@
             copy = router_copy(k)
             copy.wait_recv()
             copy.wait_send()
-        forward = remote(rt_in.at[core], rt_in.at[core], rf_send.at[0], rf_recv.at[0], sibling)
-        forward.start()
+        router_forward(core).start()
         for copy in neighbour:
             copy.wait_recv()
             copy.wait_send()
         ids_out[...] = jnp.where(core == 0, ids[...], ids_near[...])
         ids_back[...] = jnp.where(core == 0, ids_near[...], ids[...])
         gain_out[...] = jnp.where(core == 0, gain_row[...], gain_near[...])
-        forward.wait_send()
-        remote(rt_in.at[other], rt_in.at[other], rf_send.at[0], rf_recv.at[0], sibling).wait_recv()
-        for side in range(2):
-            for k in range(chips):
-                rt_bf[side, :, k * LANES : (k + 1) * LANES] = rt_in[side, k].astype(BF16)
+        round_router(core)
         for load in loads:
             load.wait()
+
+    def router_here():
+        router_forward(core).wait_send()
+        router_forward(other).wait_recv()
+        round_router(other)
 
     def down_here():
         for j in range(chips):
@@ -309,6 +316,8 @@
         own_group(0, moment, True)
         for g in range(1, group_count):
             own_group(g, moment)
+            if g == 1:
+                pl.when(moment == 0)(router_here)
             sibling_group(g - 1, moment)
         sibling_group(group_count - 1, moment)
 
@@ -334,21 +343,11 @@
         own_act = act[core]
         for i, pair in enumerate(pairs):
             dn_acc[i] = dot(own_act, down_weight(core, pair))
-        for g in range(group_count):
-            forward_copy(core, g, moment).wait_send()
-        for k in range(1, chips):
-            dispatch_copy(k, moment).wait_send()
-
-        @pl.when(jnp.logical_not(stays(moment)))
-        def _():
-            dispatch_copy(0, moment).wait_send()
-
         @pl.when(moment == 0)
         def _():
             down_here()
 
         remote(act.at[other], act.at[other], a_send.at[0], a_recv.at[0], sibling).wait_recv()
-        swap.wait_send()
         sib_act = act[other]
         landing = half * experts + expert
 
@@ -376,6 +375,16 @@
                         part_in[moment, landing, 0:sent, :] = value[0:sent, :]
 
         prepare_pick(ids_out, micro_of(section + core - moment - 1))
+
+        swap.wait_send()
+        for g in range(group_count):
+            forward_copy(core, g, moment).wait_send()
+        for k in range(1, chips):
+            dispatch_copy(k, moment).wait_send()
+
+        @pl.when(jnp.logical_not(stays(moment)))
+        def _():
+            dispatch_copy(0, moment).wait_send()
 
         for n in range(chips - 1):
             part_copy(n).wait_send()
@@ -423,6 +432,7 @@
 
     for k in range(1, chips):
         plane_copy(k, mine).start()
+    own_members = members(gid[...])
     for k in range(1, chips):
         copy = plane_copy(k, place_of(order[k], -1))
         copy.wait_recv()
@@ -456,7 +466,7 @@
     lane_row = lax.broadcasted_iota(jnp.int32, (1, LANES), 1)
     raised = jnp.where(lane_row < GROUPS, jnp.exp(DRO_RATE * group_loss), 0.0)
     weight = raised / jnp.sum(raised, axis=1, keepdims=True) * (sections * rows) / safe
-    row_weight = jnp.sum(members(gid[...]) * weight, axis=1, keepdims=True)
+    row_weight = jnp.sum(own_members * weight, axis=1, keepdims=True)
     last.wait_send()
     last.wait_recv()
     final = jnp.where(core == 0, x_all[sections].astype(F32), x_last[...].astype(F32))

time: 163 us -> 162 us (level)
  no operation moved by 1% of the time
where the time goes in v5:
time: 162 us
  Pallas kernels  159 us (98%)
  local copies, waits for them, and re-layouts  2.59 us (2%)
    pallas_call x1, Pallas kernels, per_device(): pl.pallas_call(functools.partial(kernel, sections, experts, slots, sent,...  159 us

profile of v5, /device:TPU:1, one launch (start us, length us, event | category | flops | bytes accessed | tf_op | source)
XLA Modules:
  0.0 161.8 jit_solution(1149123777325584535)
XLA Ops:
  0.6 158.6 %moe_ring.1 = (bf16[256,128]{1,0:T(8,128)(2,1)}, f32[1,8]{1,0:T(1,128)}) custom-call(bf16[256,128]{1,0:T(8,128)(2,1)} %bitcast.16, bf16[256,128]{1,0:T(8,128)(2,1)} %bitcast.17, s32[1,256]{1,0:T(1,128)} %gid_ref.1, s32[8,2,256]{2,1,0:T(2,128)} %bitcast.19, f32[1,128]{1,0:T(1,128)} %gain_ref.1, bf16[8,128]{1,0:T(8,128)(2,1)} %bitcast.20, ...), custom_call_target="tpu_custom_call" | custom-call | tf_op jit(solution)/shard_map/moe_ring/pallas_call | solution.py:561
  159.2 1.5 copy.13
  160.7 1.1 copy.14

commit v6 on v5

--- a/solution.py
+++ b/solution.py
@@ -205,16 +205,16 @@
     def dispatch(moment):
         scaled = (x_all[moment].astype(F32) * gain_out[...]).astype(BF16)
         out_buf[...] = dot(pick[...], scaled).astype(BF16)
+        @pl.when(jnp.logical_not(stays(moment)))
+        def _():
+            dispatch_copy(0, moment).start()
+
         for k in range(1, chips):
             dispatch_copy(k, moment).start()
 
         @pl.when(stays(moment))
         def _():
             x_in[moment, core, 0] = out_buf[pl.ds(pl.multiple_of(expert * slots, 16), slots), :]
-
-        @pl.when(jnp.logical_not(stays(moment)))
-        def _():
-            dispatch_copy(0, moment).start()
 
     def router_forward(source):
         return remote(rt_in.at[source], rt_in.at[source], rf_send.at[0], rf_recv.at[0], sibling)
@@ -291,7 +291,6 @@
         for k in range(max(1, groups[g][0]), groups[g][1]):
             dispatch_copy(k, moment).wait_recv()
         forward_copy(core, g, moment).start()
-        group_work(moment, core, g, fresh)
 
     def sibling_group(g, moment):
         forward_copy(other, g, moment).wait_recv()
@@ -316,10 +315,11 @@
         own_group(0, moment, True)
         for g in range(1, group_count):
             own_group(g, moment)
-            if g == 1:
-                pl.when(moment == 0)(router_here)
-            sibling_group(g - 1, moment)
-        sibling_group(group_count - 1, moment)
+        for g in range(group_count):
+            group_work(moment, core, g, g == 0)
+        pl.when(moment == 0)(router_here)
+        for g in range(group_count):
+            sibling_group(g, moment)
 
         row_scale = lax.rsqrt(jnp.sum(sq_acc[...], axis=1, keepdims=True) / width + 1e-6)
         gate_part = acc[:, 0:hidden] * row_scale

time: 162 us -> 163 us (level)
  no operation moved by 1% of the time
where the time goes in v6:
time: 163 us
  Pallas kernels  159 us (98%)
  local copies, waits for them, and re-layouts  2.59 us (2%)
    pallas_call x1, Pallas kernels, per_device(): pl.pallas_call(functools.partial(kernel, sections, experts, slots, sent,...  159 us

profile of v6, /device:TPU:1, one launch (start us, length us, event | category | flops | bytes accessed | tf_op | source)
XLA Modules:
  0.0 162.7 jit_solution(264051472662459475)
XLA Ops:
  0.6 159.5 %moe_ring.1 = (bf16[256,128]{1,0:T(8,128)(2,1)}, f32[1,8]{1,0:T(1,128)}) custom-call(bf16[256,128]{1,0:T(8,128)(2,1)} %bitcast.16, bf16[256,128]{1,0:T(8,128)(2,1)} %bitcast.17, s32[1,256]{1,0:T(1,128)} %gid_ref.1, s32[8,2,256]{2,1,0:T(2,128)} %bitcast.19, f32[1,128]{1,0:T(1,128)} %gain_ref.1, bf16[8,128]{1,0:T(8,128)(2,1)} %bitcast.20, ...), custom_call_target="tpu_custom_call" | custom-call | tf_op jit(solution)/shard_map/moe_ring/pallas_call | solution.py:561
  160.1 1.5 copy.13
  161.6 1.1 copy.14
